TPU v7x, 32 devices: a whole 2x2x4 slice. The times are simulated.
32 devices in a mesh: dp: 8 (over y, x, core), ctx: 4 (over z).
Axes of the slice: x: 2, y: 2, z: 4, core: 2. Of those that a mesh axis runs over, the one named last changes fastest.
Arguments:
- query_proj: bfloat16 [8, 512, 4096], P('dp', 'ctx'), may hold values from -6 to 6
- key_proj: bfloat16 [8, 512, 4096], P('dp', 'ctx'), may hold values from -6 to 6
- value_proj: bfloat16 [8, 512, 4096], P('dp', 'ctx'), may hold values from -6 to 6
- offsets: int32 [8, 512], P('dp', 'ctx'), may hold values from 0 to 511, as said below
- filter_taps: float32 [256, 128], P(('dp', 'ctx')), may hold values from -1.2 to 1.2
- filter_decay: float32 [256], P(('dp', 'ctx')), may hold values from 0.003125 to 0.09375
- out_weight: bfloat16 [4096, 8192], P('dp', 'ctx'), may hold values from -0.09375 to 0.09375
- grad_mixed: bfloat16 [8, 512, 8192], P('dp', None, 'ctx'), may hold values from -1.5 to 1.5
Outputs:
- mixed: bfloat16 [8, 512, 8192], P('dp', None, 'ctx')
- grad_query: bfloat16 [8, 512, 4096], P('dp', 'ctx')
- grad_key: bfloat16 [8, 512, 4096], P('dp', 'ctx')
- grad_value: bfloat16 [8, 512, 4096], P('dp', 'ctx')
- grad_weight: float32 [4096, 8192], P('dp', 'ctx')
- grad_taps: float32 [256, 128], P(('dp', 'ctx'))
- grad_decay: float32 [256], P(('dp', 'ctx'))
Inputs may be any that keep to these rules, and one draw needn't show every extreme that they name: offsets is 0 at the first base of every window and of every contig, and otherwise one more than at the base before.
All inputs are finite; a program needn't handle non-finite values.
Results may differ from a plain program's by a relative error of at most 0.02.
Values may be sent and summed in bfloat16 or wider, within the bound.
A program may use at most 192 MiB of HBM per device.

v0:
```python
import jax
import jax.numpy as jnp
from jax import lax
from jax.sharding import PartitionSpec as P


def shifted(value, axis, by):
    length = lax.axis_size(axis)
    pairs = [(i, i + by) for i in range(length) if 0 <= i + by < length]
    return lax.ppermute(value, axis, pairs)


def build_toeplitz(filter_bf, offset_loc, row_count, span_rows):
    tap_count = filter_bf.shape[1]
    group_count = filter_bf.shape[0]
    reversed_taps = filter_bf.T[::-1]
    base_rows = jnp.concatenate(
        [reversed_taps, jnp.zeros((span_rows + 1 - tap_count, group_count), jnp.bfloat16)], axis=0
    )
    tiled = jnp.tile(base_rows, (row_count, 1))[: row_count * span_rows]
    tiled = tiled.reshape(row_count, span_rows, group_count)
    out_rows = jnp.arange(row_count, dtype=jnp.int32)[:, None]
    in_rows = jnp.arange(span_rows, dtype=jnp.int32)[None, :]
    lag_index = out_rows + tap_count - 1 - in_rows
    allowed = lag_index <= offset_loc[:, None]
    return jnp.where(allowed[:, :, None], tiled, jnp.zeros((), jnp.bfloat16))


def local(
    query_proj, key_proj, value_proj, offsets, filter_taps, filter_decay, out_weight, grad_mixed
):
    query_loc = query_proj[0]
    key_loc = key_proj[0]
    value_loc = value_proj[0]
    offset_loc = offsets[0]
    cotangent = grad_mixed[0]
    row_count = query_loc.shape[0]
    chan_count = query_loc.shape[1]
    tap_count = filter_taps.shape[1]
    reach_rows = tap_count - 1
    span_rows = row_count + reach_rows
    taps_all, decay_all = (
        lax.all_gather(filter_taps, ("dp", "ctx"), axis=0, tiled=True),
        lax.all_gather(filter_decay, ("dp", "ctx"), axis=0, tiled=True),
    )
    group_count = taps_all.shape[0]
    group_width = chan_count // group_count
    tap_index = jnp.arange(tap_count, dtype=jnp.float32)
    decay_env = jnp.exp(-decay_all[:, None] * tap_index[None, :])
    filter_bf = (taps_all * decay_env).astype(jnp.bfloat16)
    mixer_in = (key_loc.astype(jnp.float32) * value_loc.astype(jnp.float32)).astype(jnp.bfloat16)
    previous = shifted(mixer_in[row_count - reach_rows :], "ctx", 1)
    mixer_ext = jnp.concatenate([previous, mixer_in], axis=0)
    toeplitz = build_toeplitz(filter_bf, offset_loc, row_count, span_rows)
    mixer3 = mixer_ext.reshape(span_rows, group_count, group_width)
    conv_out = jnp.einsum(
        "tsg,sgc->tgc", toeplitz, mixer3, preferred_element_type=jnp.float32
    ).reshape(row_count, chan_count)
    gated = (query_loc.astype(jnp.float32) * conv_out).astype(jnp.bfloat16)
    weight_full = lax.all_gather(out_weight, "dp", axis=0, tiled=True)
    gated_full = lax.all_gather(gated, "ctx", axis=0, tiled=True)
    mixed = jnp.dot(gated_full, weight_full, preferred_element_type=jnp.float32).astype(
        jnp.bfloat16
    )
    grad_gated = lax.psum_scatter(
        lax.dot_general(
            cotangent, weight_full, (((1,), (1,)), ((), ())), preferred_element_type=jnp.float32
        ).astype(jnp.bfloat16),
        "ctx",
        scatter_dimension=0,
        tiled=True,
    ).astype(jnp.float32)
    grad_query = (grad_gated * conv_out).astype(jnp.bfloat16)
    grad_conv = (grad_gated * query_loc.astype(jnp.float32)).astype(jnp.bfloat16)
    grad3 = grad_conv.reshape(row_count, group_count, group_width)
    grad_ext = jnp.einsum(
        "tsg,tgc->sgc", toeplitz, grad3, preferred_element_type=jnp.float32
    ).reshape(span_rows, chan_count)
    spill = shifted(grad_ext[:reach_rows].astype(jnp.bfloat16), "ctx", -1).astype(jnp.float32)
    grad_mixer = grad_ext[reach_rows:].at[row_count - reach_rows :].add(spill)
    grad_key = (grad_mixer * value_loc.astype(jnp.float32)).astype(jnp.bfloat16)
    grad_value = (grad_mixer * key_loc.astype(jnp.float32)).astype(jnp.bfloat16)
    block_count = 4
    block_size = group_count // block_count
    lag_keep = (reach_rows - jnp.arange(tap_count, dtype=jnp.int32))[None, :] <= offset_loc[:, None]
    pieces = []
    for block_index in range(block_count):
        low_group = block_index * block_size
        products = jnp.einsum(
            "tgc,sgc->tsg",
            grad3[:, low_group : low_group + block_size],
            mixer3[:, low_group : low_group + block_size],
            preferred_element_type=jnp.float32,
        )
        flattened = products.reshape(row_count * span_rows, block_size)
        flattened = jnp.concatenate(
            [flattened, jnp.zeros((row_count, block_size), jnp.float32)], axis=0
        )
        diagonal = flattened.reshape(row_count, span_rows + 1, block_size)[:, :tap_count]
        pieces.append(jnp.sum(jnp.where(lag_keep[:, :, None], diagonal, jnp.float32(0.0)), axis=0))
    by_lag = jnp.concatenate(pieces, axis=1)
    grad_filter = by_lag[::-1].T
    taps_part = grad_filter * decay_env
    decay_part = -jnp.sum(tap_index[None, :] * grad_filter * taps_all * decay_env, axis=1)
    grad_taps, grad_decay = (
        lax.psum_scatter(taps_part, ("dp", "ctx"), scatter_dimension=0, tiled=True),
        lax.psum_scatter(decay_part, ("dp", "ctx"), scatter_dimension=0, tiled=True),
    )
    grad_weight = lax.psum_scatter(
        lax.dot_general(
            gated_full, cotangent, (((0,), (0,)), ((), ())), preferred_element_type=jnp.float32
        ).astype(jnp.bfloat16),
        "dp",
        scatter_dimension=0,
        tiled=True,
    ).astype(jnp.float32)
    return (
        mixed[None],
        grad_query[None],
        grad_key[None],
        grad_value[None],
        grad_weight,
        grad_taps,
        grad_decay,
    )


def solution(mesh):
    in_specs = (
        P("dp", "ctx", None),
        P("dp", "ctx", None),
        P("dp", "ctx", None),
        P("dp", "ctx"),
        P(("dp", "ctx"), None),
        P(("dp", "ctx")),
        P("dp", "ctx"),
        P("dp", None, "ctx"),
    )
    out_specs = (
        P("dp", None, "ctx"),
        P("dp", "ctx", None),
        P("dp", "ctx", None),
        P("dp", "ctx", None),
        P("dp", "ctx"),
        P(("dp", "ctx"), None),
        P(("dp", "ctx")),
    )
    return jax.shard_map(local, mesh=mesh, in_specs=in_specs, out_specs=out_specs, check_vma=False)
```

profile of v0, /device:TPU:0, one launch (start us, length us, event | category | flops | bytes accessed | tf_op | source)
XLA Modules:
  0.0 786.9 jit_solution(17749648390196525107)
XLA Ops:
  8.0 94.5 %all-gather.5.cloned.1.call-done = bf16[4096,2048]{1,0:T(8,128)(2,1)} async-done(((bf16[512,2048]{1,0:T(8,128)(2,1)}), bf16[4096,2048]{1,0:T(8,128)(2,1)}) %all-gather.5.cloned.1.call-update) | async-done | bytes 16777232 | tf_op jit(solution)/shard_map/all_gather | solution.py:60
  102.5 13.8 %convolution_convert_fusion.1 = bf16[512,4096]{1,0:T(8,128)(2,1)} fusion(bf16[4096,2048]{1,0:T(8,128)(2,1)} %all-gather.5.cloned.1.call-done, bf16[1,512,2048]{2,1,0:T(8,128)(2,1)S(1)} %copy-done), kind=kOutput, calls=%fused_computation.2 | convolution fusion | flops 8592031744 | bytes 23068672 | tf_op jit(solution)/shard_map/dot_general | solution.py:66
  117.1 41.7 %all-reduce.5 = f32[256]{0:T(256)S(1)} all-reduce(f32[256]{0:T(256)S(1)} %dynamic-update-slice.3), channel_id=1, replica_groups=mesh['dp'=8,'ctx'=4] {'dp','ctx'}, use_global_device_ids=true, to_apply=%add.5 | all-reduce | flops 256 | bytes 2048
  158.8 71.1 %all_gather.12 = f32[256,128]{1,0:T(8,128)S(1)} all-gather(f32[8,128]{1,0:T(8,128)S(1)} %copy-done.11), channel_id=1, replica_groups=mesh['dp'=8,'ctx'=4] {'dp','ctx'}, dimensions={0}, use_global_device_ids=true | all-gather | bytes 135168 | tf_op jit(solution)/shard_map/all_gather | solution.py:43
  239.6 19.0 %reshape.175 = bf16[128,255,256]{2,1,0:T(8,128)(2,1)} reshape(bf16[32640,256]{1,0:T(8,128)(2,1)} %slice.93) | data formatting | bytes 33423360 | tf_op jit(solution)/shard_map/reshape | solution.py:21
  258.8 11.9 %broadcast_select_fusion = bf16[128,255,256]{2,1,0:T(8,128)(2,1)} fusion(bf16[128,255,256]{2,1,0:T(8,128)(2,1)} %reshape.175, pred[128,255]{1,0:T(8,128)(4,1)S(1)} %subtract_compare_fusion), kind=kLoop, calls=%fused_computation | loop fusion | flops 8355840 | bytes 33456000 | tf_op jit(solution)/shard_map/jit(_where)/select_n | solution.py:26
  270.7 23.3 %copy.42 = bf16[128,255,256]{1,0,2:T(8,128)(2,1)} copy(bf16[128,255,256]{2,1,0:T(8,128)(2,1)} %broadcast_select_fusion) | data formatting | bytes 33423360 | tf_op jit(solution)/shard_map/jit(_where)/select_n | solution.py:26
  298.1 7.0 convolution_bitcast_fusion.4
  323.8 9.6 %collective-permute-done.1 = bf16[127,4096]{1,0:T(8,128)(2,1)} collective-permute-done((bf16[127,4096]{1,0:T(8,128)(2,1)}, bf16[127,4096]{1,0:T(8,128)(2,1)}, u32[]{:S(2)}, u32[]{:S(2)}) %collective-permute-start.1) | collective-permute-done | bytes 1040416 | tf_op jit(solution)/shard_map/ppermute | solution.py:10
  350.2 15.7 %collective-permute-done = bf16[127,4096]{1,0:T(8,128)(2,1)S(1)} collective-permute-done((bf16[127,4096]{1,0:T(8,128)(2,1)S(1)}, bf16[127,4096]{1,0:T(8,128)(2,1)S(1)}, u32[]{:S(2)}, u32[]{:S(2)}) %collective-permute-start) | collective-permute-done | bytes 1040416 | tf_op jit(solution)/shard_map/ppermute | solution.py:10
  371.6 12.2 %fusion.24 = f32[256,16,128]{2,1,0:T(8,128)} fusion(bf16[255,256,16]{0,2,1:T(8,128)(2,1)} %bitcast.103, bf16[128,255,256]{1,0,2:T(8,128)(2,1)} %copy.42), kind=kOutput, calls=%fused_computation.56 | convolution fusion | flops 267386880 | bytes 20897792 | tf_op jit(solution)/shard_map/tsg,sgc->tgc/dot_general | solution.py:56
  405.7 9.0 %copy.50 = f32[128,255,64]{1,0,2:T(8,128)} copy(f32[128,255,64]{0,1,2:T(8,128)} %convolution_bitcast_fusion.3) | data formatting | bytes 16711680 | tf_op jit(solution)/shard_map/tgc,sgc->tsg/transpose | solution.py:89
  414.7 9.6 %reshape.179 = f32[32640,64]{0,1:T(8,128)} reshape(f32[128,255,64]{1,0,2:T(8,128)} %copy.50) | data formatting | bytes 16711680 | tf_op jit(solution)/shard_map/reshape | solution.py:95
  434.1 9.0 %copy.51 = f32[128,255,64]{1,0,2:T(8,128)} copy(f32[128,255,64]{0,1,2:T(8,128)} %convolution_bitcast_fusion.2) | data formatting | bytes 16711680 | tf_op jit(solution)/shard_map/tgc,sgc->tsg/transpose | solution.py:89
  443.2 9.3 %reshape.181 = f32[32640,64]{0,1:T(8,128)} reshape(f32[128,255,64]{1,0,2:T(8,128)} %copy.51) | data formatting | bytes 16711680 | tf_op jit(solution)/shard_map/reshape | solution.py:95
  462.2 9.0 %copy.52 = f32[128,255,64]{1,0,2:T(8,128)} copy(f32[128,255,64]{0,1,2:T(8,128)} %convolution_bitcast_fusion.1) | data formatting | bytes 16711680 | tf_op jit(solution)/shard_map/tgc,sgc->tsg/transpose | solution.py:89
  471.2 9.4 %reshape.183 = f32[32640,64]{0,1:T(8,128)} reshape(f32[128,255,64]{1,0,2:T(8,128)} %copy.52) | data formatting | bytes 16711680 | tf_op jit(solution)/shard_map/reshape | solution.py:95
  494.9 9.0 %copy.53 = f32[128,255,64]{1,0,2:T(8,128)} copy(f32[128,255,64]{0,1,2:T(8,128)} %convolution_bitcast_fusion) | data formatting | bytes 16711680 | tf_op jit(solution)/shard_map/tgc,sgc->tsg/transpose | solution.py:89
  503.9 9.2 %reshape.185 = f32[32640,64]{0,1:T(8,128)} reshape(f32[128,255,64]{1,0,2:T(8,128)} %copy.53) | data formatting | bytes 16711680 | tf_op jit(solution)/shard_map/reshape | solution.py:95
  530.7 14.9 %convolution_convert_fusion = bf16[4096,2048]{1,0:T(8,128)(2,1)} fusion(bf16[512,4096]{1,0:T(8,128)(2,1)} %all-gather.3.cloned.1.call-done, bf16[1,512,2048]{2,1,0:T(8,128)(2,1)S(1)} %copy-done), kind=kOutput, calls=%fused_computation.1 | convolution fusion | flops 8598323200 | bytes 23068672 | tf_op jit(solution)/shard_map/dot_general | solution.py:110
  545.6 44.6 %all-reduce.7 = f32[256]{0:T(256)S(1)} all-reduce(f32[256]{0:T(256)S(1)} %neg.8), channel_id=5, replica_groups=mesh['dp'=8,'ctx'=4] {'dp','ctx'}, use_global_device_ids=true, to_apply=%region_8.9.clone | all-reduce | flops 256 | bytes 2048
  590.8 66.2 %all-reduce.10.cloned.1.call-done = f32[256,128]{1,0:T(8,128)} async-done(((f32[256,128]{1,0:T(8,128)}), f32[256,128]{1,0:T(8,128)}) %all-reduce.10.cloned.1.call-update) | async-done | bytes 131088
  658.2 14.5 %fusion.4 = bf16[1,512,2048]{2,1,0:T(8,128)(2,1)} fusion(bf16[512,4096]{1,0:T(8,128)(2,1)} %all-gather.3.cloned.1.call-done, bf16[4096,2048]{1,0:T(8,128)(2,1)} %all-gather.5.cloned.1.call-done), kind=kOutput, calls=%fused_computation.16 | convolution fusion | flops 8590983168 | bytes 23068672 | tf_op jit(solution)/shard_map/dot_general | solution.py:62
  672.8 103.0 %reduce-scatter.5.cloned.1.call-done = bf16[512,2048]{1,0:T(8,128)(2,1)} async-done(((bf16[4096,2048]{1,0:T(8,128)(2,1)}), bf16[512,2048]{1,0:T(8,128)(2,1)}) %reduce-scatter.5.cloned.1.call-update) | async-done | bytes 2097168 | tf_op jit(solution)/shard_map/reduce_scatter | solution.py:109
  (96 shorter events, 135.8 us)
Async XLA Ops:
  7.2 95.3 %copy-start = (bf16[1,512,2048]{2,1,0:T(8,128)(2,1)S(1)}, bf16[1,512,2048]{2,1,0:T(8,128)(2,1)}, u32[]{:S(2)}) copy-start(bf16[1,512,2048]{2,1,0:T(8,128)(2,1)} %param.17) | copy-start | bytes 6291460
  7.2 95.3 %all-gather.5.cloned.1.call-start = ((), (), s32[]{:S(2)}) async-start(), calls=%async_computation.3 | async-start | bytes 18874368 | tf_op jit(solution)/shard_map/all_gather | solution.py:60
  7.9 286.1 %reduce-scatter.3.cloned.1.call-start = ((), (), s32[]{:S(2)}) async-start(), calls=%async_computation.4 | async-start | bytes 5242880 | tf_op jit(solution)/shard_map/reduce_scatter | solution.py:65
  116.3 0.7 copy-start.13
  116.3 42.5 %copy-start.11 = (f32[8,128]{1,0:T(8,128)S(1)}, f32[8,128]{1,0:T(8,128)}, u32[]{:S(2)}) copy-start(f32[8,128]{1,0:T(8,128)} %param.14) | copy-start | bytes 12292
  116.3 414.4 %all-gather.3.cloned.1.call-start = ((), (), s32[]{:S(2)}) async-start(), calls=%async_computation.2 | async-start | bytes 5242880 | tf_op jit(solution)/shard_map/all_gather | solution.py:61
  158.8 71.1 %copy-start.9 = (f32[256]{0:T(256)}, f32[256]{0:T(256)S(1)}, u32[]{:S(2)}) copy-start(f32[256]{0:T(256)S(1)} %neg.7) | copy-start | bytes 3076
  229.9 0.6 copy-start.6
  239.6 19.0 %copy-start.12 = (s32[1,128]{1,0:T(1,128)S(1)}, s32[1,128]{1,0:T(1,128)}, u32[]{:S(2)}) copy-start(s32[1,128]{1,0:T(1,128)} %param.13) | copy-start | bytes 1540
  270.7 23.3 %copy-start.5 = (bf16[1,128,4096]{2,1,0:T(8,128)(2,1)S(1)}, bf16[1,128,4096]{2,1,0:T(8,128)(2,1)}, u32[]{:S(2)}) copy-start(bf16[1,128,4096]{2,1,0:T(8,128)(2,1)} %param.10) | copy-start | bytes 3145732
  305.1 2.0 copy-start.1
  310.7 5.7 copy-start.2
  310.7 22.7 %collective-permute-start.1 = (bf16[127,4096]{1,0:T(8,128)(2,1)}, bf16[127,4096]{1,0:T(8,128)(2,1)}, u32[]{:S(2)}, u32[]{:S(2)}) collective-permute-start(bf16[127,4096]{1,0:T(8,128)(2,1)} %copy.47), channel_id=1, source_target_pairs={{1,0},{2,1},{3,2},{5,4},{6,5},{7,6},{9,8},{10,9},{11,10},{13,12},{... | collective-permute-start | bytes 3121160 | tf_op jit(solution)/shard_map/ppermute | solution.py:10
  347.5 18.4 %collective-permute-start = (bf16[127,4096]{1,0:T(8,128)(2,1)S(1)}, bf16[127,4096]{1,0:T(8,128)(2,1)S(1)}, u32[]{:S(2)}, u32[]{:S(2)}) collective-permute-start(bf16[127,4096]{1,0:T(8,128)(2,1)S(1)} %slice.92), channel_id=1, source_target_pairs={{0,1},{1,2},{2,3},{4,5},{5,6},{6,7},{8,9},{9,10},{10,11},{12,13},{... | collective-permute-start | bytes 3121160 | tf_op jit(solution)/shard_map/ppermute | solution.py:10
  383.8 5.7 copy-start.3
  405.5 251.5 %all-reduce.10.cloned.1.call-start = ((), (), s32[]{:S(2)}) async-start(), calls=%async_computation.6 | async-start | bytes 262144
  484.7 5.7 copy-start.4
  513.2 9.9 %slice-start = ((s8[8388608]{0:T(1024)(128)(4,1)}), s8[4194304]{0:T(1024)(128)(4,1)S(1)}, s32[]{:S(2)}) async-start(s8[8388608]{0:T(1024)(128)(4,1)} %bitcast.97), calls=%async_computation.7 | async-start | bytes 8388608
  517.4 5.7 slice-start.1
  517.4 5.7 copy-start.8
  523.1 6.7 copy-start.7
  523.1 6.7 copy-start.10
  530.6 245.2 %reduce-scatter.5.cloned.1.call-start = ((), (), s32[]{:S(2)}) async-start(), calls=%async_computation.5 | async-start | bytes 18874368 | tf_op jit(solution)/shard_map/reduce_scatter | solution.py:109
Sparse Core Ops, SparseCore 0:
  9.9 92.5 all-gather.4
  116.4 79.0 reduce-scatter.2
  405.6 84.6 all-gather.2
  530.7 126.1 all-reduce.9
  660.8 114.9 reduce-scatter.4
where the time goes:
time: 798 us; the launch traced here: 787 us
  waiting for transfers between devices  290 us (36%)
  local copies, waits for them, and re-layouts  200 us (25%)
  blocking collectives  157 us (20%)
  matrix products  81.6 us (10%)
  other arithmetic  39.9 us (5%)
  between operations  14.5 us (2%)
    reduce_scatter x1, waiting for transfers between devices, local(): lax.psum_scatter(lax.dot_general(gated_full, cotangent, (((0,), (0,)), ((...  103 us
    all_gather x1, waiting for transfers between devices, local(): weight_full = lax.all_gather(out_weight, 'dp', axis=0, tiled=True)  94.5 us
    unnamed x2, blocking collectives  86.2 us
    all_gather x1, blocking collectives, local(): lax.all_gather(filter_taps, ('dp', 'ctx'), axis=0, tiled=True)  71.1 us
    unnamed x6, waiting for transfers between devices  66.9 us
    reshape x4, local copies, waits for them, and re-layouts, local(): flattened = products.reshape(row_count * span_rows, block_size)  37.6 us
    transpose x4, local copies, waits for them, and re-layouts, local(): jnp.einsum('tgc,sgc->tsg', grad3[:, low_group:low_group + block_size], mi...  36 us
    unnamed x41, local copies, waits for them, and re-layouts  28.3 us
  transfers between devices with their start and end apart: 7, of which 5 were waited for; matrix products, arithmetic and copies ran while one was open for 29% of the time, Pallas kernels for 0%

commit v1 on v0

v1 whole, which is shorter than its diff:
```python
import functools

import jax
import jax.numpy as jnp
from jax import lax
from jax.experimental import pallas as pl
from jax.experimental.pallas import tpu as pltpu
from jax.sharding import PartitionSpec as P

MESH = pl.DeviceIdType.MESH
F32 = jnp.float32
BF16 = jnp.bfloat16
LANES = 128


def greet(n_dp, n_ctx, me_dp, me_ctx):
    barrier = pltpu.get_barrier_semaphore()
    for step in range(1, n_ctx):
        peer = (me_dp, lax.rem(me_ctx + step, n_ctx))
        pl.semaphore_signal(barrier, inc=1, device_id=peer, device_id_type=MESH)
    for step in range(1, n_dp):
        peer = (lax.rem(me_dp + step, n_dp), me_ctx)
        pl.semaphore_signal(barrier, inc=1, device_id=peer, device_id_type=MESH)
    pl.semaphore_wait(barrier, n_ctx + n_dp - 2)


def gather_kernel(n_dp, n_ctx, x_ref, out_ref, held, send1, recv1, send2, recv2):
    me_dp, me_ctx = lax.axis_index("dp"), lax.axis_index("ctx")
    greet(n_dp, n_ctx, me_dp, me_ctx)
    held[me_dp, me_ctx] = x_ref[...]
    copies = []
    for step in range(1, n_ctx):
        copy = pltpu.make_async_remote_copy(
            src_ref=x_ref,
            dst_ref=held.at[me_dp, me_ctx],
            send_sem=send1.at[step - 1],
            recv_sem=recv1.at[step - 1],
            device_id=(me_dp, lax.rem(me_ctx + step, n_ctx)),
            device_id_type=MESH,
        )
        copy.start()
        copies.append(copy)
    for copy in copies:
        copy.wait()
    copies = []
    for step in range(1, n_dp):
        copy = pltpu.make_async_remote_copy(
            src_ref=held.at[me_dp],
            dst_ref=held.at[me_dp],
            send_sem=send2.at[step - 1],
            recv_sem=recv2.at[step - 1],
            device_id=(lax.rem(me_dp + step, n_dp), me_ctx),
            device_id_type=MESH,
        )
        copy.start()
        copies.append(copy)
    for copy in copies:
        copy.wait()
    out_ref[...] = held[...]


def gather_filters(filter_loc, n_dp, n_ctx):
    rows, taps = filter_loc.shape
    out = pl.pallas_call(
        functools.partial(gather_kernel, n_dp, n_ctx),
        out_shape=jax.ShapeDtypeStruct((n_dp, n_ctx, rows, taps), F32),
        in_specs=[pl.BlockSpec(memory_space=pltpu.VMEM)],
        out_specs=pl.BlockSpec(memory_space=pltpu.VMEM),
        scratch_shapes=[
            pltpu.VMEM((n_dp, n_ctx, rows, taps), F32),
            pltpu.SemaphoreType.DMA((n_ctx - 1,)),
            pltpu.SemaphoreType.DMA((n_ctx - 1,)),
            pltpu.SemaphoreType.DMA((n_dp - 1,)),
            pltpu.SemaphoreType.DMA((n_dp - 1,)),
        ],
        compiler_params=pltpu.CompilerParams(collective_id=0, has_side_effects=True),
    )(filter_loc)
    return out.reshape(n_dp * n_ctx * rows, taps)


def reduce_kernel(n_dp, n_ctx, x_ref, out_ref, got1, part, got2, send1, recv1, send2, recv2):
    me_dp, me_ctx = lax.axis_index("dp"), lax.axis_index("ctx")
    greet(n_dp, n_ctx, me_dp, me_ctx)
    copies = []
    for step in range(1, n_ctx):
        peer = lax.rem(me_ctx + step, n_ctx)
        copy = pltpu.make_async_remote_copy(
            src_ref=x_ref.at[peer],
            dst_ref=got1.at[step - 1],
            send_sem=send1.at[step - 1],
            recv_sem=recv1.at[step - 1],
            device_id=(me_dp, peer),
            device_id_type=MESH,
        )
        copy.start()
        copies.append(copy)
    for copy in copies:
        copy.wait()
    total = x_ref[me_ctx]
    for step in range(1, n_ctx):
        total = total + got1[step - 1]
    part[...] = total
    copies = []
    for step in range(1, n_dp):
        peer = lax.rem(me_dp + step, n_dp)
        copy = pltpu.make_async_remote_copy(
            src_ref=part.at[peer],
            dst_ref=got2.at[step - 1],
            send_sem=send2.at[step - 1],
            recv_sem=recv2.at[step - 1],
            device_id=(peer, me_ctx),
            device_id_type=MESH,
        )
        copy.start()
        copies.append(copy)
    for copy in copies:
        copy.wait()
    total = part[me_dp]
    for step in range(1, n_dp):
        total = total + got2[step - 1]
    out_ref[...] = total


def reduce_filters(grad_filter, n_dp, n_ctx):
    groups, taps = grad_filter.shape
    rows = groups // (n_dp * n_ctx)
    blocks = grad_filter.reshape(n_dp, n_ctx, rows, taps).transpose(1, 0, 2, 3)
    return pl.pallas_call(
        functools.partial(reduce_kernel, n_dp, n_ctx),
        out_shape=jax.ShapeDtypeStruct((rows, taps), F32),
        in_specs=[pl.BlockSpec(memory_space=pltpu.VMEM)],
        out_specs=pl.BlockSpec(memory_space=pltpu.VMEM),
        scratch_shapes=[
            pltpu.VMEM((n_ctx - 1, n_dp, rows, taps), F32),
            pltpu.VMEM((n_dp, rows, taps), F32),
            pltpu.VMEM((n_dp - 1, rows, taps), F32),
            pltpu.SemaphoreType.DMA((n_ctx - 1,)),
            pltpu.SemaphoreType.DMA((n_ctx - 1,)),
            pltpu.SemaphoreType.DMA((n_dp - 1,)),
            pltpu.SemaphoreType.DMA((n_dp - 1,)),
        ],
        compiler_params=pltpu.CompilerParams(collective_id=1, has_side_effects=True),
    )(blocks)


def circulant(row):
    size = row.shape[1]
    return pltpu.roll(
        jnp.broadcast_to(row, (size, size)), 0, 1, stride=1, stride_axis=0
    )


def grids(size):
    return (
        lax.broadcasted_iota(jnp.int32, (size, size), 0),
        lax.broadcasted_iota(jnp.int32, (size, size), 1),
    )


def forward_kernel(width, off_ref, filt_ref, prev_ref, mix_ref, query_ref, conv_ref, gated_ref):
    size = LANES
    t_index, u_index = grids(size)
    off = jnp.broadcast_to(off_ref[...], (size, size))
    own = (u_index <= t_index) & (t_index - u_index <= off)
    before = (u_index > t_index) & (t_index + size - u_index <= off)
    per_tile = LANES // width
    lane_group = lax.broadcasted_iota(jnp.int32, (2 * size, LANES), 1) // width
    for tile in range(mix_ref.shape[1] // LANES):
        cols = slice(tile * LANES, (tile + 1) * LANES)
        mixer = jnp.concatenate([prev_ref[:, cols], mix_ref[:, cols]], axis=0)
        total = jnp.zeros((size, LANES), F32)
        for index in range(per_tile):
            group = tile * per_tile + index
            ring = circulant(filt_ref[group : group + 1, :])
            band = jnp.concatenate(
                [jnp.where(before, ring, 0.0).astype(BF16), jnp.where(own, ring, 0.0).astype(BF16)],
                axis=1,
            )
            picked = jnp.where(lane_group == index, mixer, jnp.zeros((), BF16))
            total = total + jnp.dot(band, picked, preferred_element_type=F32)
        conv_ref[:, cols] = total
        gated_ref[:, cols] = (query_ref[:, cols].astype(F32) * total).astype(BF16)


def conv_forward(offset_col, filt_rev, previous, mixer_in, query, width, block):
    rows, chans = mixer_in.shape
    groups = block // width
    spec = pl.BlockSpec((rows, block), lambda i: (0, i))
    return pl.pallas_call(
        functools.partial(forward_kernel, width),
        grid=(chans // block,),
        out_shape=(
            jax.ShapeDtypeStruct((rows, chans), F32),
            jax.ShapeDtypeStruct((rows, chans), BF16),
        ),
        in_specs=[
            pl.BlockSpec((rows, 1), lambda i: (0, 0)),
            pl.BlockSpec((groups, rows), lambda i: (i, 0)),
            spec,
            spec,
            spec,
        ],
        out_specs=(spec, spec),
        cost_estimate=pl.CostEstimate(
            flops=4 * rows * rows * LANES * (chans // width),
            bytes_accessed=12 * rows * chans,
            transcendentals=0,
        ),
    )(offset_col, filt_rev, previous, mixer_in, query)


def backward_kernel(
    width, parts, off_row_ref, off_flip_ref, filt_ref, prev_ref, mix_ref, query_ref, conv_ref, *rest
):
    part_refs = rest[:parts]
    gquery_ref, gmix_ref, spill_ref, gfilt_ref = rest[parts:]
    size = LANES
    u_index, t_index = grids(size)
    off = jnp.broadcast_to(off_row_ref[...], (size, size))
    own = (u_index <= t_index) & (t_index - u_index <= off)
    before = (u_index > t_index) & (t_index + size - u_index <= off)
    flip_row, lag_col = grids(size)
    flip_t = size - 1 - flip_row
    off_flip = jnp.broadcast_to(off_flip_ref[...], (size, size))
    own_flip = (lag_col <= flip_t) & (flip_t - lag_col <= off_flip)
    before_flip = (lag_col > flip_t) & (flip_t + size - lag_col <= off_flip)
    flip = jnp.where(flip_row + lag_col == size - 1, 1.0, 0.0).astype(BF16)
    per_tile = LANES // width
    lane_group = lax.broadcasted_iota(jnp.int32, (size, LANES), 1) // width
    zero = jnp.zeros((), BF16)
    for tile in range(mix_ref.shape[1] // LANES):
        cols = slice(tile * LANES, (tile + 1) * LANES)
        mixer = jnp.concatenate([prev_ref[:, cols], mix_ref[:, cols]], axis=0)
        gated_grad = part_refs[0][:, cols].astype(F32)
        for ref in part_refs[1:]:
            gated_grad = gated_grad + ref[:, cols].astype(F32)
        gquery_ref[:, cols] = (gated_grad * conv_ref[:, cols]).astype(BF16)
        gconv = (gated_grad * query_ref[:, cols].astype(F32)).astype(BF16)
        flipped = jnp.dot(flip, gconv, preferred_element_type=F32).astype(BF16)
        total = jnp.zeros((2 * size, LANES), F32)
        for pair in range(per_tile // 2):
            bands, picks = [], []
            for index in (2 * pair, 2 * pair + 1):
                group = tile * per_tile + index
                ring = circulant(filt_ref[group : group + 1, :])
                bands.append(
                    jnp.concatenate(
                        [
                            jnp.where(before, ring, 0.0).astype(BF16),
                            jnp.where(own, ring, 0.0).astype(BF16),
                        ],
                        axis=0,
                    )
                )
                picks.append(jnp.where(lane_group == index, gconv, zero))
                product = lax.dot_general(
                    jnp.where(lane_group == index, flipped, zero),
                    mixer,
                    (((1,), (1,)), ((), ())),
                    preferred_element_type=F32,
                )
                folded = jnp.where(
                    own_flip,
                    product[:, size:],
                    jnp.where(before_flip, product[:, :size], 0.0),
                )
                aligned = pltpu.roll(folded, 1, 1, stride=1, stride_axis=0)
                gfilt_ref[group : group + 1, :] = jnp.sum(aligned, axis=0, keepdims=True)
            total = total + jnp.dot(
                jnp.concatenate(bands, axis=1),
                jnp.concatenate(picks, axis=0),
                preferred_element_type=F32,
            )
        spill_ref[:, cols] = total[:size].astype(BF16)
        gmix_ref[:, cols] = total[size:]


def conv_backward(
    offset_row, offset_flip, filt, previous, mixer_in, query, conv_out, parts, width, block
):
    rows, chans = mixer_in.shape
    groups = block // width
    spec = pl.BlockSpec((rows, block), lambda i: (0, i))
    filt_spec = pl.BlockSpec((groups, rows), lambda i: (i, 0))
    return pl.pallas_call(
        functools.partial(backward_kernel, width, len(parts)),
        grid=(chans // block,),
        out_shape=(
            jax.ShapeDtypeStruct((rows, chans), BF16),
            jax.ShapeDtypeStruct((rows, chans), F32),
            jax.ShapeDtypeStruct((rows, chans), BF16),
            jax.ShapeDtypeStruct((chans // width, rows), F32),
        ),
        in_specs=[
            pl.BlockSpec((1, rows), lambda i: (0, 0)),
            pl.BlockSpec((rows, 1), lambda i: (0, 0)),
            filt_spec,
            spec,
            spec,
            spec,
            spec,
        ]
        + [spec] * len(parts),
        out_specs=(spec, spec, spec, filt_spec),
        cost_estimate=pl.CostEstimate(
            flops=8 * rows * rows * LANES * (chans // width),
            bytes_accessed=28 * rows * chans,
            transcendentals=0,
        ),
    )(offset_row, offset_flip, filt, previous, mixer_in, query, conv_out, *parts)


def shifted(value, axis, by):
    length = lax.axis_size(axis)
    pairs = [(i, i + by) for i in range(length) if 0 <= i + by < length]
    return lax.ppermute(value, axis, pairs)


def rotated(value, axis, by):
    length = lax.axis_size(axis)
    return lax.ppermute(value, axis, [(i, (i + by) % length) for i in range(length)])


def mirror(rows):
    return jnp.concatenate([rows[:, :1], rows[:, :0:-1]], axis=1)


def local(
    query_proj, key_proj, value_proj, offsets, filter_taps, filter_decay, out_weight, grad_mixed
):
    n_dp, n_ctx = lax.axis_size("dp"), lax.axis_size("ctx")
    me_ctx = lax.axis_index("ctx")
    query_loc = query_proj[0]
    key_loc = key_proj[0]
    value_loc = value_proj[0]
    offset_loc = offsets[0]
    cotangent = grad_mixed[0]
    rows, chans = query_loc.shape
    taps = filter_taps.shape[1]

    weight_full = lax.all_gather(out_weight, "dp", axis=0, tiled=True)
    mixer_in = (key_loc.astype(F32) * value_loc.astype(F32)).astype(BF16)
    previous = shifted(mixer_in, "ctx", 1)

    tap_index = jnp.arange(taps, dtype=F32)
    decay_env = jnp.exp(-filter_decay[:, None] * tap_index[None, :])
    filter_loc = (filter_taps * decay_env).astype(BF16).astype(F32)
    filt = gather_filters(filter_loc, n_dp, n_ctx)
    width = chans // filt.shape[0]
    block = 2 * LANES

    conv_out, gated = conv_forward(
        offset_loc[:, None], mirror(filt), previous, mixer_in, query_loc, width, block
    )
    gated_full = lax.dynamic_update_slice(
        jnp.zeros((n_ctx * rows, chans), BF16), gated, (me_ctx * rows, 0)
    )
    for step in range(1, n_ctx):
        came = rotated(gated, "ctx", step)
        source = lax.rem(me_ctx - step + n_ctx, n_ctx)
        gated_full = lax.dynamic_update_slice(gated_full, came, (source * rows, 0))

    grad_part = lax.dot_general(
        cotangent, weight_full, (((1,), (1,)), ((), ())), preferred_element_type=F32
    ).astype(BF16)
    parts = [lax.dynamic_slice(grad_part, (me_ctx * rows, 0), (rows, chans))]
    for step in range(1, n_ctx):
        target = lax.rem(me_ctx + step, n_ctx)
        sent = lax.dynamic_slice(grad_part, (target * rows, 0), (rows, chans))
        parts.append(rotated(sent, "ctx", step))

    grad_weight = lax.psum_scatter(
        lax.dot_general(
            gated_full, cotangent, (((0,), (0,)), ((), ())), preferred_element_type=F32
        ).astype(BF16),
        "dp",
        scatter_dimension=0,
        tiled=True,
    ).astype(F32)
    mixed = jnp.dot(gated_full, weight_full, preferred_element_type=F32).astype(BF16)

    grad_query, grad_own, spill, lag_sums = conv_backward(
        offset_loc[None, :],
        offset_loc[::-1][:, None],
        filt,
        previous,
        mixer_in,
        query_loc,
        conv_out,
        parts,
        width,
        block,
    )
    grad_mixer = grad_own + shifted(spill, "ctx", -1).astype(F32)
    grad_key = (grad_mixer * value_loc.astype(F32)).astype(BF16)
    grad_value = (grad_mixer * key_loc.astype(F32)).astype(BF16)

    grad_filter = mirror(reduce_filters(lag_sums, n_dp, n_ctx))
    grad_taps = grad_filter * decay_env
    grad_decay = -jnp.sum(tap_index[None, :] * grad_filter * filter_taps * decay_env, axis=1)
    return (
        mixed[None],
        grad_query[None],
        grad_key[None],
        grad_value[None],
        grad_weight,
        grad_taps,
        grad_decay,
    )


def solution(mesh):
    in_specs = (
        P("dp", "ctx", None),
        P("dp", "ctx", None),
        P("dp", "ctx", None),
        P("dp", "ctx"),
        P(("dp", "ctx"), None),
        P(("dp", "ctx")),
        P("dp", "ctx"),
        P("dp", None, "ctx"),
    )
    out_specs = (
        P("dp", None, "ctx"),
        P("dp", "ctx", None),
        P("dp", "ctx", None),
        P("dp", "ctx", None),
        P("dp", "ctx"),
        P(("dp", "ctx"), None),
        P(("dp", "ctx")),
    )
    return jax.shard_map(local, mesh=mesh, in_specs=in_specs, out_specs=out_specs, check_vma=False)
```

time: 798 us -> 360 us (0.45); the launches traced: 787 us -> 358 us
  local copies, waits for them, and re-layouts: 200 us -> 11.1 us
  blocking collectives: 157 us -> 0 us
  waiting for transfers between devices: 290 us -> 164 us
  Pallas kernels: 0 us -> 76.2 us
  matrix products: 81.6 us -> 39.6 us
  starting transfers between devices: 3.9 us -> 38.7 us
  other arithmetic: 39.9 us -> 14.4 us
    all_gather x1, waiting for transfers between devices: 94.5 us -> 0.02 us  [local(): weight_full = lax.all_gather(out_weight, 'dp', axis=0, tiled=True)]
    unnamed x2 -> x0, blocking collectives: 86.2 us -> none
    pallas_call x0 -> x4, Pallas kernels: none -> 76.2 us  [the longest x1 25.8 us: gather_filters(): pl.pallas_call(functools.partial(gather_kernel, n_dp, n_ctx), out_shape=j...]
    all_gather x1 -> x0, blocking collectives: 71.1 us -> none  [local(): lax.all_gather(filter_taps, ('dp', 'ctx'), axis=0, tiled=True)]
    unnamed x6 -> x2, waiting for transfers between devices: 66.9 us -> 0.7 us
    ppermute x0 -> x6, waiting for transfers between devices: none -> 65.4 us  [rotated(): lax.ppermute(value, axis, [(i, (i + by) % length) for i in range(length)])]
    reshape x6 -> x1, local copies, waits for them, and re-layouts: 59.5 us -> 0.66 us  [reduce_filters(): blocks = grad_filter.reshape(n_dp, n_ctx, rows, taps).transpose(1, 0, 2, 3)]
    dot_general x7 -> x1, matrix products: 53 us -> 14.7 us  [local(): jnp.dot(gated_full, weight_full, preferred_element_type=F32).astype(BF16)]
  transfers between devices with their start and end apart: 7 -> 10, of which waited for: 5 -> 3; matrix products, arithmetic and copies ran while one was open for 29% -> 16% of each run, Pallas kernels for 0% -> 16%
where the time goes in v1:
time: 360 us; the launch traced here: 358 us
  waiting for transfers between devices  164 us (46%)
  Pallas kernels  76.2 us (21%)
  matrix products  39.6 us (11%)
  starting transfers between devices  38.7 us (11%)
  other arithmetic  14.4 us (4%)
  between operations  14.2 us (4%)
  local copies, waits for them, and re-layouts  11.1 us (3%)
    reduce_scatter x1, waiting for transfers between devices, local(): lax.psum_scatter(lax.dot_general(gated_full, cotangent, (((0,), (0,)), ((...  97.6 us
    ppermute x6, waiting for transfers between devices, rotated(): lax.ppermute(value, axis, [(i, (i + by) % length) for i in range(length)])  65.4 us
    ppermute x6, starting transfers between devices, rotated(): lax.ppermute(value, axis, [(i, (i + by) % length) for i in range(length)])  31.3 us
    pallas_call x1, Pallas kernels, gather_filters(): pl.pallas_call(functools.partial(gather_kernel, n_dp, n_ctx), out_shape=j...  25.8 us
    pallas_call x1, Pallas kernels, conv_backward(): pl.pallas_call(functools.partial(backward_kernel, width, len(parts)), gri...  19.2 us
    pallas_call x1, Pallas kernels, reduce_filters(): pl.pallas_call(functools.partial(reduce_kernel, n_dp, n_ctx), out_shape=j...  17.5 us
    dot_general x1, matrix products, local(): jnp.dot(gated_full, weight_full, preferred_element_type=F32).astype(BF16)  14.7 us
    pallas_call x1, Pallas kernels, conv_forward(): pl.pallas_call(functools.partial(forward_kernel, width), grid=(chans // b...  13.7 us
  transfers between devices with their start and end apart: 10, of which 3 were waited for; matrix products, arithmetic and copies ran while one was open for 16% of the time, Pallas kernels for 16%

profile of v1, /device:TPU:0, one launch (start us, length us, event | category | flops | bytes accessed | tf_op | source)
XLA Modules:
  0.0 358.0 jit_solution(8870055105144311343)
XLA Ops:
  8.0 1.8 fusion.2.mix_ref
  9.8 5.9 %collective-permute-start = (bf16[128,4096]{1,0:T(8,128)(2,1)S(1)}, bf16[128,4096]{1,0:T(8,128)(2,1)}, u32[]{:S(2)}, u32[]{:S(2)}) collective-permute-start(bf16[128,4096]{1,0:T(8,128)(2,1)S(1)} %fusion.2.mix_ref), channel_id=1, source_target_pairs={{0,1},{1,2},{2,3},{4,5},{5,6},{6,7},{8,9},{9,10},{10,11},{12,13},{... | collective-permute-start | bytes 3145736 | tf_op jit(solution)/shard_map/ppermute | solution.py:316
  17.1 25.8 %shard_map.135 = f32[8,4,8,128]{3,2,1,0:T(8,128)} custom-call(f32[8,128]{1,0:T(8,128)} %fusion.9.x_ref), custom_call_target="tpu_custom_call" | custom-call | tf_op jit(solution)/shard_map/pallas_call | solution.py:64
  44.1 1.7 pad_maximum_fusion.filt_ref
  45.8 13.7 %shard_map.136 = (f32[128,4096]{1,0:T(8,128)}, bf16[128,4096]{1,0:T(8,128)(2,1)}) custom-call(s32[128,1]{1,0:T(8,128)} %copy.17.off_ref, f32[256,128]{1,0:T(8,128)} %pad_maximum_fusion.filt_ref, bf16[128,4096]{1,0:T(8,128)(2,1)} %collective-permute-done.prev_ref, bf16[128,4096]{1,0:T(8,128)(2,1)} %copy-done.4, bf16[128,4096]{1,0:T(8,128)(2,1)} %bitcast.44), custom_call_target="tpu_custom_call" | custom-call | flops 2147483648 | bytes 6291456 | tf_op jit(solution)/shard_map/pallas_call | solution.py:189
  59.5 2.5 collective-permute-start.1
  62.0 2.6 collective-permute-start.2
  64.6 1.4 collective-permute-start.3
  66.7 21.8 %collective-permute-done.1 = bf16[128,4096]{1,0:T(8,128)(2,1)} collective-permute-done((bf16[128,4096]{1,0:T(8,128)(2,1)}, bf16[128,4096]{1,0:T(8,128)(2,1)}, u32[]{:S(2)}, u32[]{:S(2)}) %collective-permute-start.1) | collective-permute-done | bytes 1048608 | tf_op jit(solution)/shard_map/ppermute | solution.py:321
  89.9 43.6 %collective-permute-done.2 = bf16[128,4096]{1,0:T(8,128)(2,1)} collective-permute-done((bf16[128,4096]{1,0:T(8,128)(2,1)}, bf16[128,4096]{1,0:T(8,128)(2,1)}, u32[]{:S(2)}, u32[]{:S(2)}) %collective-permute-start.2) | collective-permute-done | bytes 1048608 | tf_op jit(solution)/shard_map/ppermute | solution.py:321
  134.9 2.1 copy-done.3
  137.0 12.5 %convolution_convert_fusion = bf16[4096,2048]{1,0:T(8,128)(2,1)} fusion(bf16[512,4096]{1,0:T(8,128)(2,1)S(1)} %constant_dynamic-update-slice_fusion, bf16[1,512,2048]{2,1,0:T(8,128)(2,1)S(1)} %copy-done), kind=kOutput, calls=%fused_computation | convolution fusion | flops 8598323200 | bytes 23068672 | tf_op jit(solution)/shard_map/dot_general | solution.py:373
  149.5 12.5 %convolution_convert_fusion.1 = bf16[512,4096]{1,0:T(8,128)(2,1)S(1)} fusion(bf16[4096,2048]{1,0:T(8,128)(2,1)} %all-gather.2.cloned.1.call-done, bf16[1,512,2048]{2,1,0:T(8,128)(2,1)S(1)} %copy-done), kind=kOutput, calls=%fused_computation.1 | convolution fusion | flops 8592031744 | bytes 23068672 | tf_op jit(solution)/shard_map/dot_general | solution.py:363
  162.0 1.3 constant_dynamic-slice_fusion
  163.3 21.5 %collective-permute-start.4 = (bf16[128,4096]{1,0:T(8,128)(2,1)S(1)}, bf16[128,4096]{1,0:T(8,128)(2,1)}, u32[]{:S(2)}, u32[]{:S(2)}) collective-permute-start(bf16[128,4096]{1,0:T(8,128)(2,1)S(1)} %get-tuple-element.21), channel_id=1, source_target_pairs={{0,1},{1,2},{2,3},{3,0},{4,5},{5,6},{6,7},{7,4},{8,9},{9,10},{10,1... | collective-permute-start | bytes 3145736 | tf_op jit(solution)/shard_map/ppermute | solution.py:321
  184.8 3.2 collective-permute-start.5
  188.8 97.6 %reduce-scatter.2.cloned.1.call-done = bf16[512,2048]{1,0:T(8,128)(2,1)} async-done(((bf16[4096,2048]{1,0:T(8,128)(2,1)}), bf16[512,2048]{1,0:T(8,128)(2,1)}) %reduce-scatter.2.cloned.1.call-update) | async-done | bytes 2097168 | tf_op jit(solution)/shard_map/reduce_scatter | solution.py:372
  286.5 4.1 %convert_element_type.57 = f32[512,2048]{1,0:T(8,128)} convert(bf16[512,2048]{1,0:T(8,128)(2,1)} %reduce-scatter.2.cloned.1.call-done) | non-fusion elementwise | flops 1048576 | bytes 6291456 | tf_op jit(solution)/shard_map/convert_element_type | solution.py:379
  290.6 19.2 %shard_map.137 = (bf16[128,4096]{1,0:T(8,128)(2,1)}, f32[128,4096]{1,0:T(8,128)}, bf16[128,4096]{1,0:T(8,128)(2,1)}, f32[256,128]{1,0:T(8,128)}) custom-call(s32[1,128]{1,0:T(1,128)} %off_row_ref.1, s32[128,1]{1,0:T(8,128)} %copy.18.off_flip_ref, f32[256,128]{1,0:T(8,128)} %bitcast.37, bf16[128,4096]{1,0:T(8,128)(2,1)} %collective-permute-done.prev_ref, ...), custom_call_target="tpu_custom_call" | custom-call | flops 4294967296 | bytes 14680064 | tf_op jit(solution)/shard_map/pallas_call | solution.py:285
  309.8 1.4 collective-permute-start.7
  311.3 14.7 %fusion = bf16[1,512,2048]{2,1,0:T(8,128)(2,1)} fusion(bf16[512,4096]{1,0:T(8,128)(2,1)} %copy-done.3, bf16[4096,2048]{1,0:T(8,128)(2,1)} %all-gather.2.cloned.1.call-done), kind=kOutput, calls=%fused_computation.3 | convolution fusion | flops 8590983168 | bytes 23068672 | tf_op jit(solution)/shard_map/dot_general | solution.py:380
  326.6 17.5 %shard_map.138 = f32[8,128]{1,0:T(8,128)} custom-call(f32[4,8,8,128]{3,2,1,0:T(8,128)} %bitcast.38), custom_call_target="tpu_custom_call" | custom-call | tf_op jit(solution)/shard_map/pallas_call | solution.py:128
  345.0 1.5 multiply_reduce_fusion
  347.0 4.2 %fusion.6 = (bf16[1,128,4096]{2,1,0:T(8,128)(2,1)}, bf16[1,128,4096]{2,1,0:T(8,128)(2,1)}) fusion(f32[128,4096]{1,0:T(8,128)} %get-tuple-element.16, bf16[128,4096]{1,0:T(8,128)(2,1)} %collective-permute-done.7, bf16[1,128,4096]{2,1,0:T(8,128)(2,1)S(1)} %copy-done.2, bf16[1,128,4096]{2,1,0:T(8,128)(2,1)} %param.10), kind=kLoop, calls=%fused_computation.13 | loop fusion | flops 4194304 | bytes 7340032 | tf_op jit(solution)/shard_map/broadcast_in_dim | solution.py:405
  (47 shorter events, 9.7 us)
Async XLA Ops:
  7.2 129.8 %copy-start = (bf16[1,512,2048]{2,1,0:T(8,128)(2,1)S(1)}, bf16[1,512,2048]{2,1,0:T(8,128)(2,1)}, u32[]{:S(2)}) copy-start(bf16[1,512,2048]{2,1,0:T(8,128)(2,1)} %param.15) | copy-start | bytes 6291460
  7.2 8.5 %copy-start.8 = (s32[1,128]{1,0:T(1,128)S(1)}, s32[1,128]{1,0:T(1,128)}, u32[]{:S(2)}) copy-start(s32[1,128]{1,0:T(1,128)} %off_row_ref.1) | copy-start | bytes 1540
  7.2 9.3 %copy-start.9 = (f32[8]{0:T(128)S(1)}, f32[8]{0:T(128)}, u32[]{:S(2)}) copy-start(f32[8]{0:T(128)} %param.13) | copy-start | bytes 100
  7.2 9.3 %copy-start.7 = (f32[8,128]{1,0:T(8,128)S(1)}, f32[8,128]{1,0:T(8,128)}, u32[]{:S(2)}) copy-start(f32[8,128]{1,0:T(8,128)} %param.12) | copy-start | bytes 12292
  7.2 142.3 %all-gather.2.cloned.1.call-start = ((), (), s32[]{:S(2)}) async-start(), calls=%async_computation.1 | async-start | bytes 18874368 | tf_op jit(solution)/shard_map/all_gather | solution.py:341
  8.0 278.5 %reduce-scatter.2.cloned.1.call-start = ((), (), s32[]{:S(2)}) async-start(), calls=%async_computation.2 | async-start | bytes 18874368 | tf_op jit(solution)/shard_map/reduce_scatter | solution.py:372
  9.8 36.0 %copy-start.4 = (bf16[128,4096]{1,0:T(8,128)(2,1)}, bf16[128,4096]{1,0:T(8,128)(2,1)S(1)}, u32[]{:S(2)}) copy-start(bf16[128,4096]{1,0:T(8,128)(2,1)S(1)} %fusion.2.mix_ref) | copy-start | bytes 3145732
  9.8 36.0 %collective-permute-start = (bf16[128,4096]{1,0:T(8,128)(2,1)S(1)}, bf16[128,4096]{1,0:T(8,128)(2,1)}, u32[]{:S(2)}, u32[]{:S(2)}) collective-permute-start(bf16[128,4096]{1,0:T(8,128)(2,1)S(1)} %fusion.2.mix_ref), channel_id=1, source_target_pairs={{0,1},{1,2},{2,3},{4,5},{5,6},{6,7},{8,9},{9,10},{10,11},{12,13},{... | collective-permute-start | bytes 3145736 | tf_op jit(solution)/shard_map/ppermute | solution.py:316
  59.5 7.1 %copy-start.5 = (bf16[128,4096]{1,0:T(8,128)(2,1)S(1)}, bf16[128,4096]{1,0:T(8,128)(2,1)}, u32[]{:S(2)}) copy-start(bf16[128,4096]{1,0:T(8,128)(2,1)} %get-tuple-element.13) | copy-start | bytes 3145732
  59.5 29.0 %collective-permute-start.1 = (bf16[128,4096]{1,0:T(8,128)(2,1)}, bf16[128,4096]{1,0:T(8,128)(2,1)}, u32[]{:S(2)}, u32[]{:S(2)}) collective-permute-start(bf16[128,4096]{1,0:T(8,128)(2,1)} %get-tuple-element.13), channel_id=1, source_target_pairs={{0,1},{1,2},{2,3},{3,0},{4,5},{5,6},{6,7},{7,4},{8,9},{9,10},{10,1... | collective-permute-start | bytes 3145736 | tf_op jit(solution)/shard_map/ppermute | solution.py:321
  62.0 71.4 %collective-permute-start.2 = (bf16[128,4096]{1,0:T(8,128)(2,1)}, bf16[128,4096]{1,0:T(8,128)(2,1)}, u32[]{:S(2)}, u32[]{:S(2)}) collective-permute-start(bf16[128,4096]{1,0:T(8,128)(2,1)} %get-tuple-element.13), channel_id=1, source_target_pairs={{0,2},{1,3},{2,0},{3,1},{4,6},{5,7},{6,4},{7,5},{8,10},{9,11},{10,... | collective-permute-start | bytes 3145736 | tf_op jit(solution)/shard_map/ppermute | solution.py:321
  64.6 70.2 %collective-permute-start.3 = (bf16[128,4096]{1,0:T(8,128)(2,1)}, bf16[128,4096]{1,0:T(8,128)(2,1)S(1)}, u32[]{:S(2)}, u32[]{:S(2)}) collective-permute-start(bf16[128,4096]{1,0:T(8,128)(2,1)} %get-tuple-element.13), channel_id=1, source_target_pairs={{0,3},{1,0},{2,1},{3,2},{4,7},{5,4},{6,5},{7,6},{8,11},{9,8},{10,9... | collective-permute-start | bytes 3145736 | tf_op jit(solution)/shard_map/ppermute | solution.py:321
  134.9 2.1 copy-start.3
  163.3 127.3 %collective-permute-start.4 = (bf16[128,4096]{1,0:T(8,128)(2,1)S(1)}, bf16[128,4096]{1,0:T(8,128)(2,1)}, u32[]{:S(2)}, u32[]{:S(2)}) collective-permute-start(bf16[128,4096]{1,0:T(8,128)(2,1)S(1)} %get-tuple-element.21), channel_id=1, source_target_pairs={{0,1},{1,2},{2,3},{3,0},{4,5},{5,6},{6,7},{7,4},{8,9},{9,10},{10,1... | collective-permute-start | bytes 3145736 | tf_op jit(solution)/shard_map/ppermute | solution.py:321
  184.8 105.8 %collective-permute-start.5 = (bf16[128,4096]{1,0:T(8,128)(2,1)S(1)}, bf16[128,4096]{1,0:T(8,128)(2,1)}, u32[]{:S(2)}, u32[]{:S(2)}) collective-permute-start(bf16[128,4096]{1,0:T(8,128)(2,1)S(1)} %get-tuple-element.20), channel_id=1, source_target_pairs={{0,2},{1,3},{2,0},{3,1},{4,6},{5,7},{6,4},{7,5},{8,10},{9,11},{10,... | collective-permute-start | bytes 3145736 | tf_op jit(solution)/shard_map/ppermute | solution.py:321
  188.0 102.6 %collective-permute-start.6 = (bf16[128,4096]{1,0:T(8,128)(2,1)S(1)}, bf16[128,4096]{1,0:T(8,128)(2,1)}, u32[]{:S(2)}, u32[]{:S(2)}) collective-permute-start(bf16[128,4096]{1,0:T(8,128)(2,1)S(1)} %get-tuple-element.19), channel_id=1, source_target_pairs={{0,3},{1,0},{2,1},{3,2},{4,7},{5,4},{6,5},{7,6},{8,11},{9,8},{10,9... | collective-permute-start | bytes 3145736 | tf_op jit(solution)/shard_map/ppermute | solution.py:321
  309.8 16.2 %copy-start.6 = (f32[256,128]{1,0:T(8,128)S(1)}, f32[256,128]{1,0:T(8,128)}, u32[]{:S(2)}) copy-start(f32[256,128]{1,0:T(8,128)} %get-tuple-element.18) | copy-start | bytes 393220
  309.8 37.2 %copy-start.2 = (bf16[1,128,4096]{2,1,0:T(8,128)(2,1)S(1)}, bf16[1,128,4096]{2,1,0:T(8,128)(2,1)}, u32[]{:S(2)}) copy-start(bf16[1,128,4096]{2,1,0:T(8,128)(2,1)} %param.9) | copy-start | bytes 3145732
  309.8 37.1 %collective-permute-start.7 = (bf16[128,4096]{1,0:T(8,128)(2,1)}, bf16[128,4096]{1,0:T(8,128)(2,1)}, u32[]{:S(2)}, u32[]{:S(2)}) collective-permute-start(bf16[128,4096]{1,0:T(8,128)(2,1)} %get-tuple-element.17), channel_id=1, source_target_pairs={{1,0},{2,1},{3,2},{5,4},{6,5},{7,6},{9,8},{10,9},{11,10},{13,12},{... | collective-permute-start | bytes 3145736 | tf_op jit(solution)/shard_map/ppermute | solution.py:316
  311.3 39.9 %copy-start.1 = (bf16[1,512,2048]{2,1,0:T(8,128)(2,1)S(1)}, bf16[1,512,2048]{2,1,0:T(8,128)(2,1)}, u32[]{:S(2)}) copy-start(bf16[1,512,2048]{2,1,0:T(8,128)(2,1)} %param.15) | copy-start | bytes 6291460
Sparse Core Ops, SparseCore 0:
  9.9 94.0 all-gather.1
  149.6 136.8 reduce-scatter.1

commit v2 on v1

--- a/solution.py
+++ b/solution.py
@@ -352,13 +352,7 @@
     conv_out, gated = conv_forward(
         offset_loc[:, None], mirror(filt), previous, mixer_in, query_loc, width, block
     )
-    gated_full = lax.dynamic_update_slice(
-        jnp.zeros((n_ctx * rows, chans), BF16), gated, (me_ctx * rows, 0)
-    )
-    for step in range(1, n_ctx):
-        came = rotated(gated, "ctx", step)
-        source = lax.rem(me_ctx - step + n_ctx, n_ctx)
-        gated_full = lax.dynamic_update_slice(gated_full, came, (source * rows, 0))
+    came = [rotated(gated, "ctx", step) for step in range(1, n_ctx)]
 
     grad_part = lax.dot_general(
         cotangent, weight_full, (((1,), (1,)), ((), ())), preferred_element_type=F32
@@ -369,15 +363,21 @@
         sent = lax.dynamic_slice(grad_part, (target * rows, 0), (rows, chans))
         parts.append(rotated(sent, "ctx", step))
 
-    grad_weight = lax.psum_scatter(
-        lax.dot_general(
-            gated_full, cotangent, (((0,), (0,)), ((), ())), preferred_element_type=F32
-        ).astype(BF16),
-        "dp",
-        scatter_dimension=0,
-        tiled=True,
-    ).astype(F32)
+    gated, _ = lax.optimization_barrier((gated, grad_part))
+    gated_full = lax.dynamic_update_slice(
+        jnp.zeros((n_ctx * rows, chans), BF16), gated, (me_ctx * rows, 0)
+    )
+    for step in range(1, n_ctx):
+        source = lax.rem(me_ctx - step + n_ctx, n_ctx)
+        gated_full = lax.dynamic_update_slice(gated_full, came[step - 1], (source * rows, 0))
+
+    weight_part = lax.dot_general(
+        gated_full, cotangent, (((0,), (0,)), ((), ())), preferred_element_type=F32
+    ).astype(BF16)
+    gated_full, weight_part = lax.optimization_barrier((gated_full, weight_part))
+    weight_sum = lax.psum_scatter(weight_part, "dp", scatter_dimension=0, tiled=True)
     mixed = jnp.dot(gated_full, weight_full, preferred_element_type=F32).astype(BF16)
+    mixed, parts = lax.optimization_barrier((mixed, parts))
 
     grad_query, grad_own, spill, lag_sums = conv_backward(
         offset_loc[None, :],
@@ -398,6 +398,10 @@
     grad_filter = mirror(reduce_filters(lag_sums, n_dp, n_ctx))
     grad_taps = grad_filter * decay_env
     grad_decay = -jnp.sum(tap_index[None, :] * grad_filter * filter_taps * decay_env, axis=1)
+    weight_sum, grad_key, grad_value, grad_decay = lax.optimization_barrier(
+        (weight_sum, grad_key, grad_value, grad_decay)
+    )
+    grad_weight = weight_sum.astype(F32)
     return (
         mixed[None],
         grad_query[None],

time: 360 us -> 343 us (0.953)
  waiting for transfers between devices: 164 us -> 104 us
  Pallas kernels: 76.2 us -> 113 us
  local copies, waits for them, and re-layouts: 11.1 us -> 16.3 us
    reduce_scatter x1, waiting for transfers between devices: 97.6 us -> 0.01 us  [local(): lax.psum_scatter(weight_part, 'dp', scatter_dimension=0, tiled=True)]
    all_gather x1, waiting for transfers between devices: 0.02 us -> 37.2 us  [local(): weight_full = lax.all_gather(out_weight, 'dp', axis=0, tiled=True)]
    pallas_call x1, Pallas kernels: 17.5 us -> 52.8 us  [reduce_filters(): pl.pallas_call(functools.partial(reduce_kernel, n_dp, n_ctx), out_shape=j...]
    convert_element_type x1 -> x2, other arithmetic: 4.13 us -> 8.44 us  [the longest x1 4.31 us: local(): grad_value = (grad_mixer * key_loc.astype(F32)).astype(BF16)]
    broadcast_in_dim x1 -> x0, other arithmetic: 4.16 us -> none  [local(): grad_value[None]]
  transfers between devices with their start and end apart: 10 -> 10, of which waited for: 3 -> 4; matrix products, arithmetic and copies ran while one was open for 16% -> 15% of each run, Pallas kernels for 16% -> 33%
where the time goes in v2:
time: 343 us; the launch traced here: 342 us
  Pallas kernels  113 us (33%)
  waiting for transfers between devices  104 us (30%)
  matrix products  41.4 us (12%)
  starting transfers between devices  38.5 us (11%)
  local copies, waits for them, and re-layouts  16.3 us (5%)
  other arithmetic  14.5 us (4%)
  between operations  14.2 us (4%)
    ppermute x6, waiting for transfers between devices, rotated(): lax.ppermute(value, axis, [(i, (i + by) % length) for i in range(length)])  66.1 us
    pallas_call x1, Pallas kernels, reduce_filters(): pl.pallas_call(functools.partial(reduce_kernel, n_dp, n_ctx), out_shape=j...  52.8 us
    all_gather x1, waiting for transfers between devices, local(): weight_full = lax.all_gather(out_weight, 'dp', axis=0, tiled=True)  37.2 us
    ppermute x6, starting transfers between devices, rotated(): lax.ppermute(value, axis, [(i, (i + by) % length) for i in range(length)])  31.2 us
    pallas_call x1, Pallas kernels, gather_filters(): pl.pallas_call(functools.partial(gather_kernel, n_dp, n_ctx), out_shape=j...  26.5 us
    pallas_call x1, Pallas kernels, conv_backward(): pl.pallas_call(functools.partial(backward_kernel, width, len(parts)), gri...  19.6 us
    dot_general x1, matrix products, local(): jnp.dot(gated_full, weight_full, preferred_element_type=F32).astype(BF16)  15.1 us
    dot_general x1, matrix products, local(): lax.dot_general(cotangent, weight_full, (((1,), (1,)), ((), ())), preferr...  13.9 us
  transfers between devices with their start and end apart: 10, of which 4 were waited for; matrix products, arithmetic and copies ran while one was open for 15% of the time, Pallas kernels for 33%

profile of v2, /device:TPU:0, one launch (start us, length us, event | category | flops | bytes accessed | tf_op | source)
XLA Modules:
  0.0 341.6 jit_solution(3831206058782652555)
XLA Ops:
  8.0 1.8 fusion.1.mix_ref
  9.8 5.9 %collective-permute-start = (bf16[128,4096]{1,0:T(8,128)(2,1)S(1)}, bf16[128,4096]{1,0:T(8,128)(2,1)}, u32[]{:S(2)}, u32[]{:S(2)}) collective-permute-start(bf16[128,4096]{1,0:T(8,128)(2,1)S(1)} %fusion.1.mix_ref), channel_id=1, source_target_pairs={{0,1},{1,2},{2,3},{4,5},{5,6},{6,7},{8,9},{9,10},{10,11},{12,13},{... | collective-permute-start | bytes 3145736 | tf_op jit(solution)/shard_map/ppermute | solution.py:316
  16.4 26.5 %shard_map.135 = f32[8,4,8,128]{3,2,1,0:T(8,128)} custom-call(f32[8,128]{1,0:T(8,128)} %fusion.6.x_ref), custom_call_target="tpu_custom_call" | custom-call | tf_op jit(solution)/shard_map/pallas_call | solution.py:64
  44.9 1.7 pad_maximum_fusion.filt_ref
  46.6 13.7 %shard_map.136 = (f32[128,4096]{1,0:T(8,128)}, bf16[128,4096]{1,0:T(8,128)(2,1)}) custom-call(s32[128,1]{1,0:T(8,128)} %copy.17.off_ref, f32[256,128]{1,0:T(8,128)} %pad_maximum_fusion.filt_ref, bf16[128,4096]{1,0:T(8,128)(2,1)} %collective-permute-done.prev_ref, bf16[128,4096]{1,0:T(8,128)(2,1)} %copy-done.5, bf16[128,4096]{1,0:T(8,128)(2,1)} %bitcast.43), custom_call_target="tpu_custom_call" | custom-call | flops 2147483648 | bytes 6291456 | tf_op jit(solution)/shard_map/pallas_call | solution.py:189
  60.3 2.4 collective-permute-start.1
  62.7 2.6 collective-permute-start.2
  66.8 37.2 %all-gather.2.cloned.1.call-done = bf16[4096,2048]{1,0:T(8,128)(2,1)} async-done(((bf16[512,2048]{1,0:T(8,128)(2,1)}), bf16[4096,2048]{1,0:T(8,128)(2,1)}) %all-gather.2.cloned.1.call-update) | async-done | bytes 16777232 | tf_op jit(solution)/shard_map/all_gather | solution.py:341
  104.0 13.9 %convolution_convert_fusion.1 = bf16[512,4096]{1,0:T(8,128)(2,1)} fusion(bf16[4096,2048]{1,0:T(8,128)(2,1)} %all-gather.2.cloned.1.call-done, bf16[1,512,2048]{2,1,0:T(8,128)(2,1)S(1)} %copy-done), kind=kOutput, calls=%fused_computation.1 | convolution fusion | flops 8592031744 | bytes 23068672 | tf_op jit(solution)/shard_map/dot_general | solution.py:357
  120.6 13.5 %collective-permute-done.2 = bf16[128,4096]{1,0:T(8,128)(2,1)} collective-permute-done((bf16[128,4096]{1,0:T(8,128)(2,1)}, bf16[128,4096]{1,0:T(8,128)(2,1)}, u32[]{:S(2)}, u32[]{:S(2)}) %collective-permute-start.2) | collective-permute-done | bytes 1048608 | tf_op jit(solution)/shard_map/ppermute | solution.py:321
  135.6 2.0 copy-done.3
  137.6 12.4 %convolution_convert_fusion = bf16[4096,2048]{1,0:T(8,128)(2,1)} fusion(bf16[512,4096]{1,0:T(8,128)(2,1)S(1)} %constant_dynamic-update-slice_fusion, bf16[1,512,2048]{2,1,0:T(8,128)(2,1)S(1)} %copy-done), kind=kOutput, calls=%fused_computation | convolution fusion | flops 8598323200 | bytes 23068672 | tf_op jit(solution)/shard_map/dot_general | solution.py:374
  150.9 3.7 %constant_dynamic-slice_fusion = (bf16[128,4096]{1,0:T(8,128)(2,1)S(1)}, bf16[128,4096]{1,0:T(8,128)(2,1)S(1)}, bf16[128,4096]{1,0:T(8,128)(2,1)S(1)}, bf16[128,4096]{1,0:T(8,128)(2,1)}) fusion(bf16[512,4096]{1,0:T(8,128)(2,1)} %convolution_convert_fusion.1, s32[]{:T(128)S(6)} %select_n.17, s32[]{:T(128)S(6)} %select_n.18, s32[]{:T(128)S(6)} %select_n.19, ...), kind=kLoop, calls=%fused_computation.20 | loop fusion | bytes 8388624 | tf_op jit(solution)/shard_map/dynamic_slice | solution.py:363
  154.6 21.5 %collective-permute-start.4 = (bf16[128,4096]{1,0:T(8,128)(2,1)S(1)}, bf16[128,4096]{1,0:T(8,128)(2,1)S(1)}, u32[]{:S(2)}, u32[]{:S(2)}) collective-permute-start(bf16[128,4096]{1,0:T(8,128)(2,1)S(1)} %get-tuple-element.45), channel_id=1, source_target_pairs={{0,1},{1,2},{2,3},{3,0},{4,5},{5,6},{6,7},{7,4},{8,9},{9,10},{10,1... | collective-permute-start | bytes 3145736 | tf_op jit(solution)/shard_map/ppermute | solution.py:321
  176.2 3.2 collective-permute-start.5
  179.4 15.1 %convolution_convert_fusion.2 = bf16[512,2048]{1,0:T(8,128)(2,1)} fusion(bf16[512,4096]{1,0:T(8,128)(2,1)S(1)} %copy-done.4, bf16[4096,2048]{1,0:T(8,128)(2,1)} %all-gather.2.cloned.1.call-done), kind=kOutput, calls=%fused_computation.2 | convolution fusion | flops 8590983168 | bytes 23068672 | tf_op jit(solution)/shard_map/dot_general | solution.py:379
  194.4 8.5 %collective-permute-done.4.rest_1_ = bf16[128,4096]{1,0:T(8,128)(2,1)S(1)} collective-permute-done((bf16[128,4096]{1,0:T(8,128)(2,1)S(1)}, bf16[128,4096]{1,0:T(8,128)(2,1)S(1)}, u32[]{:S(2)}, u32[]{:S(2)}) %collective-permute-start.4) | collective-permute-done | bytes 1048608 | tf_op jit(solution)/shard_map/ppermute | solution.py:321
  202.9 44.2 %collective-permute-done.5.rest_2_ = bf16[128,4096]{1,0:T(8,128)(2,1)S(1)} collective-permute-done((bf16[128,4096]{1,0:T(8,128)(2,1)S(1)}, bf16[128,4096]{1,0:T(8,128)(2,1)S(1)}, u32[]{:S(2)}, u32[]{:S(2)}) %collective-permute-start.5) | collective-permute-done | bytes 1048608 | tf_op jit(solution)/shard_map/ppermute | solution.py:321
  248.4 19.6 %shard_map.137 = (bf16[128,4096]{1,0:T(8,128)(2,1)}, f32[128,4096]{1,0:T(8,128)}, bf16[128,4096]{1,0:T(8,128)(2,1)}, f32[256,128]{1,0:T(8,128)}) custom-call(s32[1,128]{1,0:T(1,128)} %off_row_ref.1, s32[128,1]{1,0:T(8,128)} %copy.18.off_flip_ref, f32[256,128]{1,0:T(8,128)} %bitcast.34, bf16[128,4096]{1,0:T(8,128)(2,1)} %collective-permute-done.prev_ref, ...), custom_call_target="tpu_custom_call" | custom-call | flops 4294967296 | bytes 14680064 | tf_op jit(solution)/shard_map/pallas_call | solution.py:285
  269.2 1.6 copy.21
  270.8 52.8 %shard_map.138 = f32[8,128]{1,0:T(8,128)} custom-call(f32[4,8,8,128]{3,2,1,0:T(8,128)} %bitcast.37), custom_call_target="tpu_custom_call" | custom-call | tf_op jit(solution)/shard_map/pallas_call | solution.py:128
  324.4 1.4 fusion.5
  326.4 4.3 %fusion.2 = (bf16[128,4096]{1,0:T(8,128)(2,1)}, bf16[128,4096]{1,0:T(8,128)(2,1)}) fusion(f32[128,4096]{1,0:T(8,128)} %get-tuple-element.36, bf16[128,4096]{1,0:T(8,128)(2,1)} %collective-permute-done.7, bf16[1,128,4096]{2,1,0:T(8,128)(2,1)S(1)} %copy-done.2, bf16[1,128,4096]{2,1,0:T(8,128)(2,1)} %param.10), kind=kLoop, calls=%fused_computation.8 | loop fusion | flops 4194304 | bytes 7340032 | tf_op jit(solution)/shard_map/convert_element_type | solution.py:396
  330.7 4.1 %convert_element_type.57 = f32[512,2048]{1,0:T(8,128)} convert(bf16[512,2048]{1,0:T(8,128)(2,1)} %reduce-scatter.2.cloned.1.call-done) | non-fusion elementwise | flops 1048576 | bytes 6291456 | tf_op jit(solution)/shard_map/convert_element_type | solution.py:404
  (53 shorter events, 13.7 us)
Async XLA Ops:
  7.2 96.8 %copy-start = (bf16[1,512,2048]{2,1,0:T(8,128)(2,1)S(1)}, bf16[1,512,2048]{2,1,0:T(8,128)(2,1)}, u32[]{:S(2)}) copy-start(bf16[1,512,2048]{2,1,0:T(8,128)(2,1)} %param.15) | copy-start | bytes 6291460
  7.2 8.5 %copy-start.12 = (f32[8]{0:T(128)S(1)}, f32[8]{0:T(128)}, u32[]{:S(2)}) copy-start(f32[8]{0:T(128)} %param.13) | copy-start | bytes 100
  7.2 8.5 %copy-start.7 = (f32[8,128]{1,0:T(8,128)S(1)}, f32[8,128]{1,0:T(8,128)}, u32[]{:S(2)}) copy-start(f32[8,128]{1,0:T(8,128)} %param.12) | copy-start | bytes 12292
  7.2 36.9 %copy-start.8 = (s32[1,128]{1,0:T(1,128)S(1)}, s32[1,128]{1,0:T(1,128)}, u32[]{:S(2)}) copy-start(s32[1,128]{1,0:T(1,128)} %off_row_ref.1) | copy-start | bytes 1540
  7.2 96.8 %all-gather.2.cloned.1.call-start = ((), (), s32[]{:S(2)}) async-start(), calls=%async_computation.1 | async-start | bytes 18874368 | tf_op jit(solution)/shard_map/all_gather | solution.py:341
  8.0 322.7 %reduce-scatter.2.cloned.1.call-start = ((), (), s32[]{:S(2)}) async-start(), calls=%async_computation.2 | async-start | bytes 18874368 | tf_op jit(solution)/shard_map/reduce_scatter | solution.py:378
  9.8 36.8 %copy-start.5 = (bf16[128,4096]{1,0:T(8,128)(2,1)}, bf16[128,4096]{1,0:T(8,128)(2,1)S(1)}, u32[]{:S(2)}) copy-start(bf16[128,4096]{1,0:T(8,128)(2,1)S(1)} %fusion.1.mix_ref) | copy-start | bytes 3145732
  9.8 36.7 %collective-permute-start = (bf16[128,4096]{1,0:T(8,128)(2,1)S(1)}, bf16[128,4096]{1,0:T(8,128)(2,1)}, u32[]{:S(2)}, u32[]{:S(2)}) collective-permute-start(bf16[128,4096]{1,0:T(8,128)(2,1)S(1)} %fusion.1.mix_ref), channel_id=1, source_target_pairs={{0,1},{1,2},{2,3},{4,5},{5,6},{6,7},{8,9},{9,10},{10,11},{12,13},{... | collective-permute-start | bytes 3145736 | tf_op jit(solution)/shard_map/ppermute | solution.py:316
  60.3 59.0 %collective-permute-start.1 = (bf16[128,4096]{1,0:T(8,128)(2,1)}, bf16[128,4096]{1,0:T(8,128)(2,1)}, u32[]{:S(2)}, u32[]{:S(2)}) collective-permute-start(bf16[128,4096]{1,0:T(8,128)(2,1)} %get-tuple-element.26), channel_id=1, source_target_pairs={{0,1},{1,2},{2,3},{3,0},{4,5},{5,6},{6,7},{7,4},{8,9},{9,10},{10,1... | collective-permute-start | bytes 3145736 | tf_op jit(solution)/shard_map/ppermute | solution.py:321
  62.7 71.4 %collective-permute-start.2 = (bf16[128,4096]{1,0:T(8,128)(2,1)}, bf16[128,4096]{1,0:T(8,128)(2,1)}, u32[]{:S(2)}, u32[]{:S(2)}) collective-permute-start(bf16[128,4096]{1,0:T(8,128)(2,1)} %get-tuple-element.26), channel_id=1, source_target_pairs={{0,2},{1,3},{2,0},{3,1},{4,6},{5,7},{6,4},{7,5},{8,10},{9,11},{10,... | collective-permute-start | bytes 3145736 | tf_op jit(solution)/shard_map/ppermute | solution.py:321
  65.3 70.1 %collective-permute-start.3 = (bf16[128,4096]{1,0:T(8,128)(2,1)}, bf16[128,4096]{1,0:T(8,128)(2,1)S(1)}, u32[]{:S(2)}, u32[]{:S(2)}) collective-permute-start(bf16[128,4096]{1,0:T(8,128)(2,1)} %get-tuple-element.26), channel_id=1, source_target_pairs={{0,3},{1,0},{2,1},{3,2},{4,7},{5,4},{6,5},{7,6},{8,11},{9,8},{10,9... | collective-permute-start | bytes 3145736 | tf_op jit(solution)/shard_map/ppermute | solution.py:321
  118.0 1.2 copy-start.6
  135.6 2.0 copy-start.3
  150.9 28.4 %copy-start.4 = (bf16[512,4096]{1,0:T(8,128)(2,1)S(1)}, bf16[512,4096]{1,0:T(8,128)(2,1)}, u32[]{:S(2)}) copy-start(bf16[512,4096]{1,0:T(8,128)(2,1)} %copy-done.3) | copy-start | bytes 12582916
  154.6 48.3 %collective-permute-start.4 = (bf16[128,4096]{1,0:T(8,128)(2,1)S(1)}, bf16[128,4096]{1,0:T(8,128)(2,1)S(1)}, u32[]{:S(2)}, u32[]{:S(2)}) collective-permute-start(bf16[128,4096]{1,0:T(8,128)(2,1)S(1)} %get-tuple-element.45), channel_id=1, source_target_pairs={{0,1},{1,2},{2,3},{3,0},{4,5},{5,6},{6,7},{7,4},{8,9},{9,10},{10,1... | collective-permute-start | bytes 3145736 | tf_op jit(solution)/shard_map/ppermute | solution.py:321
  176.2 70.9 %collective-permute-start.5 = (bf16[128,4096]{1,0:T(8,128)(2,1)S(1)}, bf16[128,4096]{1,0:T(8,128)(2,1)S(1)}, u32[]{:S(2)}, u32[]{:S(2)}) collective-permute-start(bf16[128,4096]{1,0:T(8,128)(2,1)S(1)} %get-tuple-element.44), channel_id=1, source_target_pairs={{0,2},{1,3},{2,0},{3,1},{4,6},{5,7},{6,4},{7,5},{8,10},{9,11},{10,... | collective-permute-start | bytes 3145736 | tf_op jit(solution)/shard_map/ppermute | solution.py:321
  179.4 67.7 %collective-permute-start.6 = (bf16[128,4096]{1,0:T(8,128)(2,1)S(1)}, bf16[128,4096]{1,0:T(8,128)(2,1)S(1)}, u32[]{:S(2)}, u32[]{:S(2)}) collective-permute-start(bf16[128,4096]{1,0:T(8,128)(2,1)S(1)} %get-tuple-element.43), channel_id=1, source_target_pairs={{0,3},{1,0},{2,1},{3,2},{4,7},{5,4},{6,5},{7,6},{8,11},{9,8},{10,9... | collective-permute-start | bytes 3145736 | tf_op jit(solution)/shard_map/ppermute | solution.py:321
  202.9 44.2 %copy-start.9 = (bf16[128,4096]{1,0:T(8,128)(2,1)}, bf16[128,4096]{1,0:T(8,128)(2,1)S(1)}, u32[]{:S(2)}) copy-start(bf16[128,4096]{1,0:T(8,128)(2,1)S(1)} %collective-permute-done.4.rest_1_) | copy-start | bytes 3145732
  247.1 1.0 copy-start.10
  247.1 1.3 copy-start.11
  248.4 78.0 %copy-start.2 = (bf16[1,128,4096]{2,1,0:T(8,128)(2,1)S(1)}, bf16[1,128,4096]{2,1,0:T(8,128)(2,1)}, u32[]{:S(2)}) copy-start(bf16[1,128,4096]{2,1,0:T(8,128)(2,1)} %param.9) | copy-start | bytes 3145732
  267.9 58.4 %collective-permute-start.7 = (bf16[128,4096]{1,0:T(8,128)(2,1)}, bf16[128,4096]{1,0:T(8,128)(2,1)}, u32[]{:S(2)}, u32[]{:S(2)}) collective-permute-start(bf16[128,4096]{1,0:T(8,128)(2,1)} %get-tuple-element.37), channel_id=1, source_target_pairs={{1,0},{2,1},{3,2},{5,4},{6,5},{7,6},{9,8},{10,9},{11,10},{13,12},{... | collective-permute-start | bytes 3145736 | tf_op jit(solution)/shard_map/ppermute | solution.py:316
  326.4 8.4 %copy-start.1 = (bf16[1,512,2048]{2,1,0:T(8,128)(2,1)S(1)}, bf16[1,512,2048]{2,1,0:T(8,128)(2,1)}, u32[]{:S(2)}) copy-start(bf16[1,512,2048]{2,1,0:T(8,128)(2,1)} %param.15) | copy-start | bytes 6291460
Sparse Core Ops, SparseCore 0:
  9.9 94.0 all-gather.1
  150.2 136.8 reduce-scatter.1

commit v3 on v2

--- a/solution.py
+++ b/solution.py
@@ -316,9 +316,10 @@
     return lax.ppermute(value, axis, pairs)
 
 
-def rotated(value, axis, by):
-    length = lax.axis_size(axis)
-    return lax.ppermute(value, axis, [(i, (i + by) % length) for i in range(length)])
+def hop(value, by, sends):
+    length = lax.axis_size("ctx")
+    pairs = [(i, i + by) for i in range(length) if 0 <= i + by < length and sends(i)]
+    return lax.ppermute(value, "ctx", pairs)
 
 
 def mirror(rows):
@@ -352,24 +353,41 @@
     conv_out, gated = conv_forward(
         offset_loc[:, None], mirror(filt), previous, mixer_in, query_loc, width, block
     )
-    came = [rotated(gated, "ctx", step) for step in range(1, n_ctx)]
+    rights, lefts = [gated], [gated]
+    for step in range(1, n_ctx):
+        rights.append(hop(rights[-1], 1, lambda i: i >= step - 1))
+        lefts.append(hop(lefts[-1], -1, lambda i: i <= n_ctx - step))
+        if step == n_ctx - 2:
+            weight_full, rights[step], lefts[step] = lax.optimization_barrier(
+                (weight_full, rights[step], lefts[step])
+            )
 
     grad_part = lax.dot_general(
         cotangent, weight_full, (((1,), (1,)), ((), ())), preferred_element_type=F32
     ).astype(BF16)
-    parts = [lax.dynamic_slice(grad_part, (me_ctx * rows, 0), (rows, chans))]
-    for step in range(1, n_ctx):
-        target = lax.rem(me_ctx + step, n_ctx)
-        sent = lax.dynamic_slice(grad_part, (target * rows, 0), (rows, chans))
-        parts.append(rotated(sent, "ctx", step))
-
-    gated, _ = lax.optimization_barrier((gated, grad_part))
+
     gated_full = lax.dynamic_update_slice(
         jnp.zeros((n_ctx * rows, chans), BF16), gated, (me_ctx * rows, 0)
     )
     for step in range(1, n_ctx):
         source = lax.rem(me_ctx - step + n_ctx, n_ctx)
-        gated_full = lax.dynamic_update_slice(gated_full, came[step - 1], (source * rows, 0))
+        came = jnp.where(me_ctx >= step, rights[step], lefts[n_ctx - step])
+        gated_full = lax.dynamic_update_slice(gated_full, came, (source * rows, 0))
+    gated_full, grad_part = lax.optimization_barrier((gated_full, grad_part))
+
+    def block_of(index):
+        return lax.dynamic_slice(grad_part, (index * rows, 0), (rows, chans))
+
+    to_right = to_left = None
+    for step in range(1, n_ctx):
+        send_right = block_of(jnp.minimum(me_ctx + n_ctx - step, n_ctx - 1))
+        send_left = block_of(jnp.maximum(me_ctx - n_ctx + step, 0))
+        if step > 1:
+            send_right = (send_right.astype(F32) + to_right.astype(F32)).astype(BF16)
+            send_left = (send_left.astype(F32) + to_left.astype(F32)).astype(BF16)
+        to_right = hop(send_right, 1, lambda i: i <= step - 1)
+        to_left = hop(send_left, -1, lambda i: i >= n_ctx - step)
+    parts = [block_of(me_ctx), to_right, to_left]
 
     weight_part = lax.dot_general(
         gated_full, cotangent, (((0,), (0,)), ((), ())), preferred_element_type=F32

time: 343 us -> 335 us (0.977)
  Pallas kernels: 113 us -> 87 us
  starting transfers between devices: 38.5 us -> 52.1 us
  other arithmetic: 14.5 us -> 27.4 us
  waiting for transfers between devices: 104 us -> 95.8 us
    all_gather x1, waiting for transfers between devices: 37.2 us -> 0.01 us  [local(): weight_full = lax.all_gather(out_weight, 'dp', axis=0, tiled=True)]
    ppermute x6 -> x12, waiting for transfers between devices: 66.1 us -> 95.1 us  [hop(): return lax.ppermute(value, 'ctx', pairs)]
    pallas_call x1, Pallas kernels: 52.8 us -> 27.5 us  [reduce_filters(): pl.pallas_call(functools.partial(reduce_kernel, n_dp, n_ctx), out_shape=j...]
    ppermute x6 -> x12, starting transfers between devices: 31.2 us -> 44.8 us  [hop(): return lax.ppermute(value, 'ctx', pairs)]
    convert_element_type x0 -> x3, other arithmetic: none -> 6.76 us  [the longest x2 5.29 us: local(): send_left = (send_left.astype(F32) + to_left.astype(F32)).astype(BF16)]
    dynamic_update_slice x0 -> x3, other arithmetic: none -> 6.1 us  [local(): gated_full = lax.dynamic_update_slice(gated_full, came, (source * rows, 0))]
  transfers between devices with their start and end apart: 10 -> 16, of which waited for: 4 -> 7; matrix products, arithmetic and copies ran while one was open for 15% -> 18% of each run, Pallas kernels for 33% -> 26%
where the time goes in v3:
time: 335 us; the launch traced here: 333 us
  waiting for transfers between devices  95.8 us (29%)
  Pallas kernels  87 us (26%)
  starting transfers between devices  52.1 us (16%)
  matrix products  43.3 us (13%)
  other arithmetic  27.4 us (8%)
  between operations  14.3 us (4%)
  local copies, waits for them, and re-layouts  12.9 us (4%)
    ppermute x12, waiting for transfers between devices, hop(): return lax.ppermute(value, 'ctx', pairs)  95.1 us
    ppermute x12, starting transfers between devices, hop(): return lax.ppermute(value, 'ctx', pairs)  44.8 us
    pallas_call x1, Pallas kernels, reduce_filters(): pl.pallas_call(functools.partial(reduce_kernel, n_dp, n_ctx), out_shape=j...  27.5 us
    pallas_call x1, Pallas kernels, gather_filters(): pl.pallas_call(functools.partial(gather_kernel, n_dp, n_ctx), out_shape=j...  26.5 us
    pallas_call x1, Pallas kernels, conv_backward(): pl.pallas_call(functools.partial(backward_kernel, width, len(parts)), gri...  19.2 us
    dot_general x1, matrix products, local(): jnp.dot(gated_full, weight_full, preferred_element_type=F32).astype(BF16)  14.7 us
    dot_general x1, matrix products, local(): lax.dot_general(gated_full, cotangent, (((0,), (0,)), ((), ())), preferre...  14.6 us
    dot_general x1, matrix products, local(): lax.dot_general(cotangent, weight_full, (((1,), (1,)), ((), ())), preferr...  13.9 us
  transfers between devices with their start and end apart: 16, of which 7 were waited for; matrix products, arithmetic and copies ran while one was open for 18% of the time, Pallas kernels for 26%

profile of v3, /device:TPU:0, one launch (start us, length us, event | category | flops | bytes accessed | tf_op | source)
XLA Modules:
  0.0 332.8 jit_solution(17395510085271187848)
XLA Ops:
  9.8 5.9 %collective-permute-start = (bf16[128,4096]{1,0:T(8,128)(2,1)S(1)}, bf16[128,4096]{1,0:T(8,128)(2,1)}, u32[]{:S(2)}, u32[]{:S(2)}) collective-permute-start(bf16[128,4096]{1,0:T(8,128)(2,1)S(1)} %fusion.2.mix_ref), channel_id=1, source_target_pairs={{0,1},{1,2},{2,3},{4,5},{5,6},{6,7},{8,9},{9,10},{10,11},{12,13},{... | collective-permute-start | bytes 3145736 | tf_op jit(solution)/shard_map/ppermute | solution.py:316
  16.4 26.5 %shard_map.135 = f32[8,4,8,128]{3,2,1,0:T(8,128)} custom-call(f32[8,128]{1,0:T(8,128)} %fusion.7.x_ref), custom_call_target="tpu_custom_call" | custom-call | tf_op jit(solution)/shard_map/pallas_call | solution.py:64
  46.6 13.7 %shard_map.136 = (f32[128,4096]{1,0:T(8,128)}, bf16[128,4096]{1,0:T(8,128)(2,1)}) custom-call(s32[128,1]{1,0:T(8,128)} %copy.18.off_ref, f32[256,128]{1,0:T(8,128)} %pad_maximum_fusion.filt_ref, bf16[128,4096]{1,0:T(8,128)(2,1)} %collective-permute-done.prev_ref, bf16[128,4096]{1,0:T(8,128)(2,1)} %copy-done.3, bf16[128,4096]{1,0:T(8,128)(2,1)} %bitcast.45), custom_call_target="tpu_custom_call" | custom-call | flops 2147483648 | bytes 6291456 | tf_op jit(solution)/shard_map/pallas_call | solution.py:189
  60.3 5.5 %collective-permute-start.1 = (bf16[128,4096]{1,0:T(8,128)(2,1)}, bf16[128,4096]{1,0:T(8,128)(2,1)}, u32[]{:S(2)}, u32[]{:S(2)}) collective-permute-start(bf16[128,4096]{1,0:T(8,128)(2,1)} %get-tuple-element.28), channel_id=1, source_target_pairs={{0,1},{1,2},{2,3},{4,5},{5,6},{6,7},{8,9},{9,10},{10,11},{12,13},{... | collective-permute-start | bytes 3145736 | tf_op jit(solution)/shard_map/ppermute | solution.py:322
  67.0 21.3 %collective-permute-done.1 = bf16[128,4096]{1,0:T(8,128)(2,1)} collective-permute-done((bf16[128,4096]{1,0:T(8,128)(2,1)}, bf16[128,4096]{1,0:T(8,128)(2,1)}, u32[]{:S(2)}, u32[]{:S(2)}) %collective-permute-start.1) | collective-permute-done | bytes 1048608 | tf_op jit(solution)/shard_map/ppermute | solution.py:322
  90.0 3.4 %collective-permute-done.3 = bf16[128,4096]{1,0:T(8,128)(2,1)} collective-permute-done((bf16[128,4096]{1,0:T(8,128)(2,1)}, bf16[128,4096]{1,0:T(8,128)(2,1)}, u32[]{:S(2)}, u32[]{:S(2)}) %collective-permute-start.3) | collective-permute-done | bytes 1048608 | tf_op jit(solution)/shard_map/ppermute | solution.py:322
  94.8 2.5 broadcast_in_dim.21
  98.4 22.2 %collective-permute-done.4 = bf16[128,4096]{1,0:T(8,128)(2,1)} collective-permute-done((bf16[128,4096]{1,0:T(8,128)(2,1)}, bf16[128,4096]{1,0:T(8,128)(2,1)}, u32[]{:S(2)}, u32[]{:S(2)}) %collective-permute-start.4) | collective-permute-done | bytes 1048608 | tf_op jit(solution)/shard_map/ppermute | solution.py:322
  122.6 13.9 %fusion = bf16[512,4096]{1,0:T(8,128)(2,1)} fusion(bf16[4096,2048]{1,0:T(8,128)(2,1)} %all-gather.2.cloned.1.call-done, bf16[1,512,2048]{2,1,0:T(8,128)(2,1)S(1)} %copy-done), kind=kOutput, calls=%fused_computation.2 | convolution fusion | flops 8592031744 | bytes 23068672 | tf_op jit(solution)/shard_map/dot_general | solution.py:365
  136.6 10.1 %collective-permute-done.5 = bf16[128,4096]{1,0:T(8,128)(2,1)S(1)} collective-permute-done((bf16[128,4096]{1,0:T(8,128)(2,1)}, bf16[128,4096]{1,0:T(8,128)(2,1)S(1)}, u32[]{:S(2)}, u32[]{:S(2)}) %collective-permute-start.5) | collective-permute-done | bytes 1048608 | tf_op jit(solution)/shard_map/ppermute | solution.py:322
  152.8 14.6 %convolution_convert_fusion = bf16[4096,2048]{1,0:T(8,128)(2,1)} fusion(bf16[512,4096]{1,0:T(8,128)(2,1)} %select_dynamic-update-slice_fusion, bf16[1,512,2048]{2,1,0:T(8,128)(2,1)S(1)} %copy-done), kind=kOutput, calls=%fused_computation | convolution fusion | flops 8598323200 | bytes 23068672 | tf_op jit(solution)/shard_map/dot_general | solution.py:392
  167.5 3.2 constant_dynamic-slice_fusion
  171.5 3.8 %collective-permute-start.7 = (bf16[128,4096]{1,0:T(8,128)(2,1)S(1)}, bf16[128,4096]{1,0:T(8,128)(2,1)}, u32[]{:S(2)}, u32[]{:S(2)}) collective-permute-start(bf16[128,4096]{1,0:T(8,128)(2,1)S(1)} %get-tuple-element.52), channel_id=1, source_target_pairs={{0,1},{4,5},{8,9},{12,13},{16,17},{20,21},{24,25},{28,29}} | collective-permute-start | bytes 3145736 | tf_op jit(solution)/shard_map/ppermute | solution.py:322
  177.7 17.2 %collective-permute-done.7 = bf16[128,4096]{1,0:T(8,128)(2,1)} collective-permute-done((bf16[128,4096]{1,0:T(8,128)(2,1)S(1)}, bf16[128,4096]{1,0:T(8,128)(2,1)}, u32[]{:S(2)}, u32[]{:S(2)}) %collective-permute-start.7) | collective-permute-done | bytes 1048608 | tf_op jit(solution)/shard_map/ppermute | solution.py:322
  194.9 3.6 %add_convert_fusion = (bf16[128,4096]{1,0:T(8,128)(2,1)S(1)}, bf16[128,4096]{1,0:T(8,128)(2,1)}) fusion(bf16[128,4096]{1,0:T(8,128)(2,1)S(1)} %collective-permute-done.11, bf16[512,4096]{1,0:T(8,128)(2,1)} %fusion, s32[]{:T(128)S(6)} %select_n.64, bf16[128,4096]{1,0:T(8,128)(2,1)} %collective-permute-done.7, s32[]{:T(128)S(6)} %select_n.62), kind=kLoop, calls=%fused_computation.13 | loop fusion | flops 4194304 | bytes 6291464 | tf_op jit(solution)/shard_map/convert_element_type | solution.py:387
  198.5 22.0 %collective-permute-start.8 = (bf16[128,4096]{1,0:T(8,128)(2,1)}, bf16[128,4096]{1,0:T(8,128)(2,1)S(1)}, u32[]{:S(2)}, u32[]{:S(2)}) collective-permute-start(bf16[128,4096]{1,0:T(8,128)(2,1)} %get-tuple-element.50), channel_id=1, source_target_pairs={{0,1},{1,2},{4,5},{5,6},{8,9},{9,10},{12,13},{13,14},{16,17},{17,1... | collective-permute-start | bytes 3145736 | tf_op jit(solution)/shard_map/ppermute | solution.py:322
  222.7 17.3 %collective-permute-done.8 = bf16[128,4096]{1,0:T(8,128)(2,1)S(1)} collective-permute-done((bf16[128,4096]{1,0:T(8,128)(2,1)}, bf16[128,4096]{1,0:T(8,128)(2,1)S(1)}, u32[]{:S(2)}, u32[]{:S(2)}) %collective-permute-start.8) | collective-permute-done | bytes 1048608 | tf_op jit(solution)/shard_map/ppermute | solution.py:322
  241.5 4.4 %collective-permute-start.9 = (bf16[128,4096]{1,0:T(8,128)(2,1)S(1)}, bf16[128,4096]{1,0:T(8,128)(2,1)S(1)}, u32[]{:S(2)}, u32[]{:S(2)}) collective-permute-start(bf16[128,4096]{1,0:T(8,128)(2,1)S(1)} %add_convert_fusion.2), channel_id=1, source_target_pairs={{0,1},{1,2},{2,3},{4,5},{5,6},{6,7},{8,9},{9,10},{10,11},{12,13},{... | collective-permute-start | bytes 3145736 | tf_op jit(solution)/shard_map/ppermute | solution.py:322
  245.9 14.7 %convolution_convert_fusion.2 = bf16[512,2048]{1,0:T(8,128)(2,1)} fusion(bf16[512,4096]{1,0:T(8,128)(2,1)} %select_dynamic-update-slice_fusion, bf16[4096,2048]{1,0:T(8,128)(2,1)} %all-gather.2.cloned.1.call-done), kind=kOutput, calls=%fused_computation.3 | convolution fusion | flops 8590983168 | bytes 23068672 | tf_op jit(solution)/shard_map/dot_general | solution.py:397
  260.6 3.5 %collective-permute-done.9.rest_1_ = bf16[128,4096]{1,0:T(8,128)(2,1)S(1)} collective-permute-done((bf16[128,4096]{1,0:T(8,128)(2,1)S(1)}, bf16[128,4096]{1,0:T(8,128)(2,1)S(1)}, u32[]{:S(2)}, u32[]{:S(2)}) %collective-permute-start.9) | collective-permute-done | bytes 1048608 | tf_op jit(solution)/shard_map/ppermute | solution.py:322
  265.1 19.2 %shard_map.137 = (bf16[128,4096]{1,0:T(8,128)(2,1)}, f32[128,4096]{1,0:T(8,128)}, bf16[128,4096]{1,0:T(8,128)(2,1)}, f32[256,128]{1,0:T(8,128)}) custom-call(s32[1,128]{1,0:T(1,128)} %off_row_ref.1, s32[128,1]{1,0:T(8,128)} %copy.20.off_flip_ref, f32[256,128]{1,0:T(8,128)} %bitcast.36, bf16[128,4096]{1,0:T(8,128)(2,1)} %collective-permute-done.prev_ref, ...), custom_call_target="tpu_custom_call" | custom-call | flops 4294967296 | bytes 14680064 | tf_op jit(solution)/shard_map/pallas_call | solution.py:285
  287.2 27.5 %shard_map.138 = f32[8,128]{1,0:T(8,128)} custom-call(f32[4,8,8,128]{3,2,1,0:T(8,128)} %bitcast.39), custom_call_target="tpu_custom_call" | custom-call | tf_op jit(solution)/shard_map/pallas_call | solution.py:128
  317.5 4.3 %fusion.3 = (bf16[128,4096]{1,0:T(8,128)(2,1)}, bf16[128,4096]{1,0:T(8,128)(2,1)}) fusion(f32[128,4096]{1,0:T(8,128)} %get-tuple-element.42, bf16[128,4096]{1,0:T(8,128)(2,1)} %collective-permute-done.13, bf16[1,128,4096]{2,1,0:T(8,128)(2,1)S(1)} %copy-done.2, bf16[1,128,4096]{2,1,0:T(8,128)(2,1)} %param.10), kind=kLoop, calls=%fused_computation.9 | loop fusion | flops 4194304 | bytes 7340032 | tf_op jit(solution)/shard_map/convert_element_type | solution.py:414
  321.8 4.1 %convert_element_type.109 = f32[512,2048]{1,0:T(8,128)} convert(bf16[512,2048]{1,0:T(8,128)(2,1)} %reduce-scatter.2.cloned.1.call-done) | non-fusion elementwise | flops 1048576 | bytes 6291456 | tf_op jit(solution)/shard_map/convert_element_type | solution.py:422
  (62 shorter events, 33.7 us)
Async XLA Ops:
  7.2 115.4 %copy-start = (bf16[1,512,2048]{2,1,0:T(8,128)(2,1)S(1)}, bf16[1,512,2048]{2,1,0:T(8,128)(2,1)}, u32[]{:S(2)}) copy-start(bf16[1,512,2048]{2,1,0:T(8,128)(2,1)} %param.15) | copy-start | bytes 6291460
  7.2 8.5 %copy-start.9 = (f32[8]{0:T(128)S(1)}, f32[8]{0:T(128)}, u32[]{:S(2)}) copy-start(f32[8]{0:T(128)} %param.13) | copy-start | bytes 100
  7.2 8.5 %copy-start.5 = (f32[8,128]{1,0:T(8,128)S(1)}, f32[8,128]{1,0:T(8,128)}, u32[]{:S(2)}) copy-start(f32[8,128]{1,0:T(8,128)} %param.12) | copy-start | bytes 12292
  7.2 36.9 %copy-start.6 = (s32[1,128]{1,0:T(1,128)S(1)}, s32[1,128]{1,0:T(1,128)}, u32[]{:S(2)}) copy-start(s32[1,128]{1,0:T(1,128)} %off_row_ref.1) | copy-start | bytes 1540
  7.2 113.4 %all-gather.2.cloned.1.call-start = ((), (), s32[]{:S(2)}) async-start(), calls=%async_computation.1 | async-start | bytes 18874368 | tf_op jit(solution)/shard_map/all_gather | solution.py:342
  8.0 313.9 %reduce-scatter.2.cloned.1.call-start = ((), (), s32[]{:S(2)}) async-start(), calls=%async_computation.2 | async-start | bytes 18874368 | tf_op jit(solution)/shard_map/reduce_scatter | solution.py:396
  9.8 36.8 %copy-start.3 = (bf16[128,4096]{1,0:T(8,128)(2,1)}, bf16[128,4096]{1,0:T(8,128)(2,1)S(1)}, u32[]{:S(2)}) copy-start(bf16[128,4096]{1,0:T(8,128)(2,1)S(1)} %fusion.2.mix_ref) | copy-start | bytes 3145732
  9.8 36.7 %collective-permute-start = (bf16[128,4096]{1,0:T(8,128)(2,1)S(1)}, bf16[128,4096]{1,0:T(8,128)(2,1)}, u32[]{:S(2)}, u32[]{:S(2)}) collective-permute-start(bf16[128,4096]{1,0:T(8,128)(2,1)S(1)} %fusion.2.mix_ref), channel_id=1, source_target_pairs={{0,1},{1,2},{2,3},{4,5},{5,6},{6,7},{8,9},{9,10},{10,11},{12,13},{... | collective-permute-start | bytes 3145736 | tf_op jit(solution)/shard_map/ppermute | solution.py:316
  60.3 37.1 %copy-start.4 = (bf16[128,4096]{1,0:T(8,128)(2,1)S(1)}, bf16[128,4096]{1,0:T(8,128)(2,1)}, u32[]{:S(2)}) copy-start(bf16[128,4096]{1,0:T(8,128)(2,1)} %get-tuple-element.28) | copy-start | bytes 3145732
  60.3 28.1 %collective-permute-start.1 = (bf16[128,4096]{1,0:T(8,128)(2,1)}, bf16[128,4096]{1,0:T(8,128)(2,1)}, u32[]{:S(2)}, u32[]{:S(2)}) collective-permute-start(bf16[128,4096]{1,0:T(8,128)(2,1)} %get-tuple-element.28), channel_id=1, source_target_pairs={{0,1},{1,2},{2,3},{4,5},{5,6},{6,7},{8,9},{9,10},{10,11},{12,13},{... | collective-permute-start | bytes 3145736 | tf_op jit(solution)/shard_map/ppermute | solution.py:322
  65.8 27.7 %collective-permute-start.3 = (bf16[128,4096]{1,0:T(8,128)(2,1)}, bf16[128,4096]{1,0:T(8,128)(2,1)}, u32[]{:S(2)}, u32[]{:S(2)}) collective-permute-start(bf16[128,4096]{1,0:T(8,128)(2,1)} %get-tuple-element.28), channel_id=1, source_target_pairs={{1,0},{2,1},{3,2},{5,4},{6,5},{7,6},{9,8},{10,9},{11,10},{13,12},{... | collective-permute-start | bytes 3145736 | tf_op jit(solution)/shard_map/ppermute | solution.py:322
  88.4 10.0 %collective-permute-start.2 = (bf16[128,4096]{1,0:T(8,128)(2,1)}, bf16[128,4096]{1,0:T(8,128)(2,1)}, u32[]{:S(2)}, u32[]{:S(2)}) collective-permute-start(bf16[128,4096]{1,0:T(8,128)(2,1)} %collective-permute-done.1), channel_id=1, source_target_pairs={{1,2},{2,3},{5,6},{6,7},{9,10},{10,11},{13,14},{14,15},{17,18},{18... | collective-permute-start | bytes 3145736 | tf_op jit(solution)/shard_map/ppermute | solution.py:322
  93.5 27.1 %collective-permute-start.4 = (bf16[128,4096]{1,0:T(8,128)(2,1)}, bf16[128,4096]{1,0:T(8,128)(2,1)}, u32[]{:S(2)}, u32[]{:S(2)}) collective-permute-start(bf16[128,4096]{1,0:T(8,128)(2,1)} %collective-permute-done.3), channel_id=1, source_target_pairs={{1,0},{2,1},{5,4},{6,5},{9,8},{10,9},{13,12},{14,13},{17,16},{18,1... | collective-permute-start | bytes 3145736 | tf_op jit(solution)/shard_map/ppermute | solution.py:322
  120.6 26.1 %collective-permute-start.5 = (bf16[128,4096]{1,0:T(8,128)(2,1)}, bf16[128,4096]{1,0:T(8,128)(2,1)S(1)}, u32[]{:S(2)}, u32[]{:S(2)}) collective-permute-start(bf16[128,4096]{1,0:T(8,128)(2,1)} %collective-permute-done.4), channel_id=1, source_target_pairs={{1,0},{5,4},{9,8},{13,12},{17,16},{21,20},{25,24},{29,28}} | collective-permute-start | bytes 3145736 | tf_op jit(solution)/shard_map/ppermute | solution.py:322
  121.9 28.5 %collective-permute-start.6 = (bf16[128,4096]{1,0:T(8,128)(2,1)}, bf16[128,4096]{1,0:T(8,128)(2,1)S(1)}, u32[]{:S(2)}, u32[]{:S(2)}) collective-permute-start(bf16[128,4096]{1,0:T(8,128)(2,1)} %collective-permute-done.2), channel_id=1, source_target_pairs={{2,3},{6,7},{10,11},{14,15},{18,19},{22,23},{26,27},{30,31}} | collective-permute-start | bytes 3145736 | tf_op jit(solution)/shard_map/ppermute | solution.py:322
  170.6 4.7 %collective-permute-start.10 = (bf16[128,4096]{1,0:T(8,128)(2,1)S(1)}, bf16[128,4096]{1,0:T(8,128)(2,1)S(1)}, u32[]{:S(2)}, u32[]{:S(2)}) collective-permute-start(bf16[128,4096]{1,0:T(8,128)(2,1)S(1)} %get-tuple-element.51), channel_id=1, source_target_pairs={{3,2},{7,6},{11,10},{15,14},{19,18},{23,22},{27,26},{31,30}} | collective-permute-start | bytes 3145736 | tf_op jit(solution)/shard_map/ppermute | solution.py:322
  171.5 23.4 %collective-permute-start.7 = (bf16[128,4096]{1,0:T(8,128)(2,1)S(1)}, bf16[128,4096]{1,0:T(8,128)(2,1)}, u32[]{:S(2)}, u32[]{:S(2)}) collective-permute-start(bf16[128,4096]{1,0:T(8,128)(2,1)S(1)} %get-tuple-element.52), channel_id=1, source_target_pairs={{0,1},{4,5},{8,9},{12,13},{16,17},{20,21},{24,25},{28,29}} | collective-permute-start | bytes 3145736 | tf_op jit(solution)/shard_map/ppermute | solution.py:322
  177.0 17.9 %collective-permute-start.11 = (bf16[128,4096]{1,0:T(8,128)(2,1)S(1)}, bf16[128,4096]{1,0:T(8,128)(2,1)S(1)}, u32[]{:S(2)}, u32[]{:S(2)}) collective-permute-start(bf16[128,4096]{1,0:T(8,128)(2,1)S(1)} %add_convert_fusion.1), channel_id=1, source_target_pairs={{2,1},{3,2},{6,5},{7,6},{10,9},{11,10},{14,13},{15,14},{18,17},{19... | collective-permute-start | bytes 3145736 | tf_op jit(solution)/shard_map/ppermute | solution.py:322
  198.5 41.5 %collective-permute-start.8 = (bf16[128,4096]{1,0:T(8,128)(2,1)}, bf16[128,4096]{1,0:T(8,128)(2,1)S(1)}, u32[]{:S(2)}, u32[]{:S(2)}) collective-permute-start(bf16[128,4096]{1,0:T(8,128)(2,1)} %get-tuple-element.50), channel_id=1, source_target_pairs={{0,1},{1,2},{4,5},{5,6},{8,9},{9,10},{12,13},{13,14},{16,17},{17,1... | collective-permute-start | bytes 3145736 | tf_op jit(solution)/shard_map/ppermute | solution.py:322
  221.4 39.2 %collective-permute-start.12 = (bf16[128,4096]{1,0:T(8,128)(2,1)S(1)}, bf16[128,4096]{1,0:T(8,128)(2,1)S(1)}, u32[]{:S(2)}, u32[]{:S(2)}) collective-permute-start(bf16[128,4096]{1,0:T(8,128)(2,1)S(1)} %get-tuple-element.49), channel_id=1, source_target_pairs={{1,0},{2,1},{3,2},{5,4},{6,5},{7,6},{9,8},{10,9},{11,10},{13,12},{... | collective-permute-start | bytes 3145736 | tf_op jit(solution)/shard_map/ppermute | solution.py:322
  241.5 22.7 %collective-permute-start.9 = (bf16[128,4096]{1,0:T(8,128)(2,1)S(1)}, bf16[128,4096]{1,0:T(8,128)(2,1)S(1)}, u32[]{:S(2)}, u32[]{:S(2)}) collective-permute-start(bf16[128,4096]{1,0:T(8,128)(2,1)S(1)} %add_convert_fusion.2), channel_id=1, source_target_pairs={{0,1},{1,2},{2,3},{4,5},{5,6},{6,7},{8,9},{9,10},{10,11},{12,13},{... | collective-permute-start | bytes 3145736 | tf_op jit(solution)/shard_map/ppermute | solution.py:322
  265.1 52.4 %copy-start.2 = (bf16[1,128,4096]{2,1,0:T(8,128)(2,1)S(1)}, bf16[1,128,4096]{2,1,0:T(8,128)(2,1)}, u32[]{:S(2)}) copy-start(bf16[1,128,4096]{2,1,0:T(8,128)(2,1)} %param.9) | copy-start | bytes 3145732
  284.3 33.2 %collective-permute-start.13 = (bf16[128,4096]{1,0:T(8,128)(2,1)}, bf16[128,4096]{1,0:T(8,128)(2,1)}, u32[]{:S(2)}, u32[]{:S(2)}) collective-permute-start(bf16[128,4096]{1,0:T(8,128)(2,1)} %get-tuple-element.43), channel_id=1, source_target_pairs={{1,0},{2,1},{3,2},{5,4},{6,5},{7,6},{9,8},{10,9},{11,10},{13,12},{... | collective-permute-start | bytes 3145736 | tf_op jit(solution)/shard_map/ppermute | solution.py:316
  317.5 8.4 %copy-start.1 = (bf16[1,512,2048]{2,1,0:T(8,128)(2,1)S(1)}, bf16[1,512,2048]{2,1,0:T(8,128)(2,1)}, u32[]{:S(2)}) copy-start(bf16[1,512,2048]{2,1,0:T(8,128)(2,1)} %param.15) | copy-start | bytes 6291460
  (2 other events, 4.5 us)
Sparse Core Ops, SparseCore 0:
  9.9 94.0 all-gather.1
  167.6 113.5 reduce-scatter.1

commit v4 on v3

--- a/solution.py
+++ b/solution.py
@@ -366,6 +366,10 @@
         cotangent, weight_full, (((1,), (1,)), ((), ())), preferred_element_type=F32
     ).astype(BF16)
 
+    first_right = lax.dynamic_slice(grad_part, ((n_ctx - 1) * rows, 0), (rows, chans))
+    first_left = lax.dynamic_slice(grad_part, (0, 0), (rows, chans))
+    to_right = hop(first_right, 1, lambda i: i <= 0)
+    to_left = hop(first_left, -1, lambda i: i >= n_ctx - 1)
     gated_full = lax.dynamic_update_slice(
         jnp.zeros((n_ctx * rows, chans), BF16), gated, (me_ctx * rows, 0)
     )
@@ -373,18 +377,18 @@
         source = lax.rem(me_ctx - step + n_ctx, n_ctx)
         came = jnp.where(me_ctx >= step, rights[step], lefts[n_ctx - step])
         gated_full = lax.dynamic_update_slice(gated_full, came, (source * rows, 0))
-    gated_full, grad_part = lax.optimization_barrier((gated_full, grad_part))
+    gated_full, grad_part, to_right, to_left = lax.optimization_barrier(
+        (gated_full, grad_part, to_right, to_left)
+    )
 
     def block_of(index):
         return lax.dynamic_slice(grad_part, (index * rows, 0), (rows, chans))
 
-    to_right = to_left = None
-    for step in range(1, n_ctx):
+    for step in range(2, n_ctx):
         send_right = block_of(jnp.minimum(me_ctx + n_ctx - step, n_ctx - 1))
         send_left = block_of(jnp.maximum(me_ctx - n_ctx + step, 0))
-        if step > 1:
-            send_right = (send_right.astype(F32) + to_right.astype(F32)).astype(BF16)
-            send_left = (send_left.astype(F32) + to_left.astype(F32)).astype(BF16)
+        send_right = (send_right.astype(F32) + to_right.astype(F32)).astype(BF16)
+        send_left = (send_left.astype(F32) + to_left.astype(F32)).astype(BF16)
         to_right = hop(send_right, 1, lambda i: i <= step - 1)
         to_left = hop(send_left, -1, lambda i: i >= n_ctx - step)
     parts = [block_of(me_ctx), to_right, to_left]

time: 335 us -> 325 us (0.970)
  waiting for transfers between devices: 95.8 us -> 77.1 us
  starting transfers between devices: 52.1 us -> 63.6 us
    ppermute x12, waiting for transfers between devices: 95.1 us -> 76.4 us  [hop(): return lax.ppermute(value, 'ctx', pairs)]
    ppermute x12, starting transfers between devices: 44.8 us -> 56.3 us  [hop(): return lax.ppermute(value, 'ctx', pairs)]
  transfers between devices with their start and end apart: 16 -> 16, of which waited for: 7 -> 6; matrix products, arithmetic and copies ran while one was open for 18% -> 19% of each run, Pallas kernels for 26% -> 27%
where the time goes in v4:
time: 325 us; the launch traced here: 323 us
  Pallas kernels  87 us (27%)
  waiting for transfers between devices  77.1 us (24%)
  starting transfers between devices  63.6 us (20%)
  matrix products  41.9 us (13%)
  other arithmetic  27.2 us (8%)
  between operations  14.3 us (4%)
  local copies, waits for them, and re-layouts  12.2 us (4%)
    ppermute x12, waiting for transfers between devices, hop(): return lax.ppermute(value, 'ctx', pairs)  76.4 us
    ppermute x12, starting transfers between devices, hop(): return lax.ppermute(value, 'ctx', pairs)  56.3 us
    pallas_call x1, Pallas kernels, reduce_filters(): pl.pallas_call(functools.partial(reduce_kernel, n_dp, n_ctx), out_shape=j...  28.2 us
    pallas_call x1, Pallas kernels, gather_filters(): pl.pallas_call(functools.partial(gather_kernel, n_dp, n_ctx), out_shape=j...  25.8 us
    pallas_call x1, Pallas kernels, conv_backward(): pl.pallas_call(functools.partial(backward_kernel, width, len(parts)), gri...  19.3 us
    dot_general x1, matrix products, local(): jnp.dot(gated_full, weight_full, preferred_element_type=F32).astype(BF16)  14.8 us
    dot_general x1, matrix products, local(): lax.dot_general(gated_full, cotangent, (((0,), (0,)), ((), ())), preferre...  14.6 us
    pallas_call x1, Pallas kernels, conv_forward(): pl.pallas_call(functools.partial(forward_kernel, width), grid=(chans // b...  13.7 us
  transfers between devices with their start and end apart: 16, of which 6 were waited for; matrix products, arithmetic and copies ran while one was open for 19% of the time, Pallas kernels for 27%

profile of v4, /device:TPU:0, one launch (start us, length us, event | category | flops | bytes accessed | tf_op | source)
XLA Modules:
  0.0 323.3 jit_solution(15560964472987437715)
XLA Ops:
  9.8 5.9 %collective-permute-start = (bf16[128,4096]{1,0:T(8,128)(2,1)S(1)}, bf16[128,4096]{1,0:T(8,128)(2,1)}, u32[]{:S(2)}, u32[]{:S(2)}) collective-permute-start(bf16[128,4096]{1,0:T(8,128)(2,1)S(1)} %fusion.2.mix_ref), channel_id=1, source_target_pairs={{0,1},{1,2},{2,3},{4,5},{5,6},{6,7},{8,9},{9,10},{10,11},{12,13},{... | collective-permute-start | bytes 3145736 | tf_op jit(solution)/shard_map/ppermute | solution.py:316
  17.1 25.8 %shard_map.135 = f32[8,4,8,128]{3,2,1,0:T(8,128)} custom-call(f32[8,128]{1,0:T(8,128)} %fusion.7.x_ref), custom_call_target="tpu_custom_call" | custom-call | tf_op jit(solution)/shard_map/pallas_call | solution.py:64
  45.8 13.7 %shard_map.136 = (f32[128,4096]{1,0:T(8,128)}, bf16[128,4096]{1,0:T(8,128)(2,1)}) custom-call(s32[128,1]{1,0:T(8,128)} %copy.18.off_ref, f32[256,128]{1,0:T(8,128)} %pad_maximum_fusion.filt_ref, bf16[128,4096]{1,0:T(8,128)(2,1)} %collective-permute-done.prev_ref, bf16[128,4096]{1,0:T(8,128)(2,1)} %copy-done.4, bf16[128,4096]{1,0:T(8,128)(2,1)} %bitcast.45), custom_call_target="tpu_custom_call" | custom-call | flops 2147483648 | bytes 6291456 | tf_op jit(solution)/shard_map/pallas_call | solution.py:189
  60.9 6.1 %collective-permute-start.1 = (bf16[128,4096]{1,0:T(8,128)(2,1)}, bf16[128,4096]{1,0:T(8,128)(2,1)}, u32[]{:S(2)}, u32[]{:S(2)}) collective-permute-start(bf16[128,4096]{1,0:T(8,128)(2,1)} %get-tuple-element.30), channel_id=1, source_target_pairs={{0,1},{1,2},{2,3},{4,5},{5,6},{6,7},{8,9},{9,10},{10,11},{12,13},{... | collective-permute-start | bytes 3145736 | tf_op jit(solution)/shard_map/ppermute | solution.py:322
  67.0 21.3 %collective-permute-done.3 = bf16[128,4096]{1,0:T(8,128)(2,1)} collective-permute-done((bf16[128,4096]{1,0:T(8,128)(2,1)}, bf16[128,4096]{1,0:T(8,128)(2,1)}, u32[]{:S(2)}, u32[]{:S(2)}) %collective-permute-start.3) | collective-permute-done | bytes 1048608 | tf_op jit(solution)/shard_map/ppermute | solution.py:322
  91.2 2.5 broadcast_in_dim.21
  94.7 21.0 %collective-permute-done.4 = bf16[128,4096]{1,0:T(8,128)(2,1)} collective-permute-done((bf16[128,4096]{1,0:T(8,128)(2,1)}, bf16[128,4096]{1,0:T(8,128)(2,1)}, u32[]{:S(2)}, u32[]{:S(2)}) %collective-permute-start.4) | collective-permute-done | bytes 1048608 | tf_op jit(solution)/shard_map/ppermute | solution.py:322
  117.7 12.5 %fusion = bf16[512,4096]{1,0:T(8,128)(2,1)S(1)} fusion(bf16[4096,2048]{1,0:T(8,128)(2,1)} %all-gather.2.cloned.1.call-done, bf16[1,512,2048]{2,1,0:T(8,128)(2,1)S(1)} %copy-done), kind=kOutput, calls=%fused_computation.2 | convolution fusion | flops 8592031744 | bytes 23068672 | tf_op jit(solution)/shard_map/dot_general | solution.py:365
  131.2 6.7 %collective-permute-start.7 = (bf16[128,4096]{1,0:T(8,128)(2,1)S(1)}, bf16[128,4096]{1,0:T(8,128)(2,1)}, u32[]{:S(2)}, u32[]{:S(2)}) collective-permute-start(bf16[128,4096]{1,0:T(8,128)(2,1)S(1)} %get-tuple-element.56), channel_id=1, source_target_pairs={{0,1},{4,5},{8,9},{12,13},{16,17},{20,21},{24,25},{28,29}} | collective-permute-start | bytes 3145736 | tf_op jit(solution)/shard_map/ppermute | solution.py:322
  137.9 5.1 %collective-permute-done.5 = bf16[128,4096]{1,0:T(8,128)(2,1)S(1)} collective-permute-done((bf16[128,4096]{1,0:T(8,128)(2,1)}, bf16[128,4096]{1,0:T(8,128)(2,1)S(1)}, u32[]{:S(2)}, u32[]{:S(2)}) %collective-permute-start.5) | collective-permute-done | bytes 1048608 | tf_op jit(solution)/shard_map/ppermute | solution.py:322
  144.1 2.4 select_dynamic-update-slice_fusion.1
  146.6 2.4 select_dynamic-update-slice_fusion
  149.0 9.1 %collective-permute-done.7 = bf16[128,4096]{1,0:T(8,128)(2,1)} collective-permute-done((bf16[128,4096]{1,0:T(8,128)(2,1)S(1)}, bf16[128,4096]{1,0:T(8,128)(2,1)}, u32[]{:S(2)}, u32[]{:S(2)}) %collective-permute-start.7) | collective-permute-done | bytes 1048608 | tf_op jit(solution)/shard_map/ppermute | solution.py:322
  158.1 14.6 %convolution_convert_fusion = bf16[4096,2048]{1,0:T(8,128)(2,1)} fusion(bf16[512,4096]{1,0:T(8,128)(2,1)} %select_dynamic-update-slice_fusion, bf16[1,512,2048]{2,1,0:T(8,128)(2,1)S(1)} %copy-done), kind=kOutput, calls=%fused_computation | convolution fusion | flops 8598323200 | bytes 23068672 | tf_op jit(solution)/shard_map/dot_general | solution.py:396
  175.0 3.6 %add_convert_fusion = (bf16[128,4096]{1,0:T(8,128)(2,1)S(1)}, bf16[128,4096]{1,0:T(8,128)(2,1)}) fusion(bf16[128,4096]{1,0:T(8,128)(2,1)S(1)} %collective-permute-done.11, bf16[512,4096]{1,0:T(8,128)(2,1)} %copy-done.2, s32[]{:T(128)S(6)} %select_n.57, bf16[128,4096]{1,0:T(8,128)(2,1)} %collective-permute-done.7, s32[]{:T(128)S(6)} %select_n.56), kind=kLoop, calls=%fused_computation.13 | loop fusion | flops 4194304 | bytes 6291464 | tf_op jit(solution)/shard_map/convert_element_type | solution.py:391
  178.6 30.2 %collective-permute-start.9 = (bf16[128,4096]{1,0:T(8,128)(2,1)}, bf16[128,4096]{1,0:T(8,128)(2,1)S(1)}, u32[]{:S(2)}, u32[]{:S(2)}) collective-permute-start(bf16[128,4096]{1,0:T(8,128)(2,1)} %get-tuple-element.54), channel_id=1, source_target_pairs={{0,1},{1,2},{4,5},{5,6},{8,9},{9,10},{12,13},{13,14},{16,17},{17,1... | collective-permute-start | bytes 3145736 | tf_op jit(solution)/shard_map/ppermute | solution.py:322
  211.0 18.0 %collective-permute-done.9 = bf16[128,4096]{1,0:T(8,128)(2,1)S(1)} collective-permute-done((bf16[128,4096]{1,0:T(8,128)(2,1)}, bf16[128,4096]{1,0:T(8,128)(2,1)S(1)}, u32[]{:S(2)}, u32[]{:S(2)}) %collective-permute-start.9) | collective-permute-done | bytes 1048608 | tf_op jit(solution)/shard_map/ppermute | solution.py:322
  230.5 4.3 %collective-permute-start.10 = (bf16[128,4096]{1,0:T(8,128)(2,1)S(1)}, bf16[128,4096]{1,0:T(8,128)(2,1)S(1)}, u32[]{:S(2)}, u32[]{:S(2)}) collective-permute-start(bf16[128,4096]{1,0:T(8,128)(2,1)S(1)} %add_convert_fusion.2), channel_id=1, source_target_pairs={{0,1},{1,2},{2,3},{4,5},{5,6},{6,7},{8,9},{9,10},{10,11},{12,13},{... | collective-permute-start | bytes 3145736 | tf_op jit(solution)/shard_map/ppermute | solution.py:322
  234.8 14.8 %convolution_convert_fusion.2 = bf16[512,2048]{1,0:T(8,128)(2,1)} fusion(bf16[512,4096]{1,0:T(8,128)(2,1)} %select_dynamic-update-slice_fusion, bf16[4096,2048]{1,0:T(8,128)(2,1)} %all-gather.2.cloned.1.call-done), kind=kOutput, calls=%fused_computation.3 | convolution fusion | flops 8590983168 | bytes 23068672 | tf_op jit(solution)/shard_map/dot_general | solution.py:401
  249.7 2.3 constant_dynamic-slice_fusion.rest_0_
  254.8 19.3 %shard_map.137 = (bf16[128,4096]{1,0:T(8,128)(2,1)}, f32[128,4096]{1,0:T(8,128)}, bf16[128,4096]{1,0:T(8,128)(2,1)}, f32[256,128]{1,0:T(8,128)}) custom-call(s32[1,128]{1,0:T(1,128)} %off_row_ref.1, s32[128,1]{1,0:T(8,128)} %copy.20.off_flip_ref, f32[256,128]{1,0:T(8,128)} %bitcast.36, bf16[128,4096]{1,0:T(8,128)(2,1)} %collective-permute-done.prev_ref, ...), custom_call_target="tpu_custom_call" | custom-call | flops 4294967296 | bytes 14680064 | tf_op jit(solution)/shard_map/pallas_call | solution.py:285
  277.0 28.2 %shard_map.138 = f32[8,128]{1,0:T(8,128)} custom-call(f32[4,8,8,128]{3,2,1,0:T(8,128)} %bitcast.39), custom_call_target="tpu_custom_call" | custom-call | tf_op jit(solution)/shard_map/pallas_call | solution.py:128
  308.0 4.3 %fusion.3 = (bf16[128,4096]{1,0:T(8,128)(2,1)}, bf16[128,4096]{1,0:T(8,128)(2,1)}) fusion(f32[128,4096]{1,0:T(8,128)} %get-tuple-element.46, bf16[128,4096]{1,0:T(8,128)(2,1)} %collective-permute-done.13, bf16[1,128,4096]{2,1,0:T(8,128)(2,1)S(1)} %copy-done.3, bf16[1,128,4096]{2,1,0:T(8,128)(2,1)} %param.10), kind=kLoop, calls=%fused_computation.9 | loop fusion | flops 4194304 | bytes 7340032 | tf_op jit(solution)/shard_map/convert_element_type | solution.py:418
  312.3 4.1 %convert_element_type.109 = f32[512,2048]{1,0:T(8,128)} convert(bf16[512,2048]{1,0:T(8,128)(2,1)} %reduce-scatter.2.cloned.1.call-done) | non-fusion elementwise | flops 1048576 | bytes 6291456 | tf_op jit(solution)/shard_map/convert_element_type | solution.py:426
  (65 shorter events, 30.8 us)
Async XLA Ops:
  7.2 110.6 %copy-start = (bf16[1,512,2048]{2,1,0:T(8,128)(2,1)S(1)}, bf16[1,512,2048]{2,1,0:T(8,128)(2,1)}, u32[]{:S(2)}) copy-start(bf16[1,512,2048]{2,1,0:T(8,128)(2,1)} %param.15) | copy-start | bytes 6291460
  7.2 8.5 %copy-start.10 = (f32[8]{0:T(128)S(1)}, f32[8]{0:T(128)}, u32[]{:S(2)}) copy-start(f32[8]{0:T(128)} %param.13) | copy-start | bytes 100
  7.2 8.5 %copy-start.7 = (s32[1,128]{1,0:T(1,128)S(1)}, s32[1,128]{1,0:T(1,128)}, u32[]{:S(2)}) copy-start(s32[1,128]{1,0:T(1,128)} %off_row_ref.1) | copy-start | bytes 1540
  7.2 9.2 %copy-start.6 = (f32[8,128]{1,0:T(8,128)S(1)}, f32[8,128]{1,0:T(8,128)}, u32[]{:S(2)}) copy-start(f32[8,128]{1,0:T(8,128)} %param.12) | copy-start | bytes 12292
  7.2 108.5 %all-gather.2.cloned.1.call-start = ((), (), s32[]{:S(2)}) async-start(), calls=%async_computation.1 | async-start | bytes 18874368 | tf_op jit(solution)/shard_map/all_gather | solution.py:342
  8.0 304.4 %reduce-scatter.2.cloned.1.call-start = ((), (), s32[]{:S(2)}) async-start(), calls=%async_computation.2 | async-start | bytes 18874368 | tf_op jit(solution)/shard_map/reduce_scatter | solution.py:400
  9.8 36.0 %copy-start.4 = (bf16[128,4096]{1,0:T(8,128)(2,1)}, bf16[128,4096]{1,0:T(8,128)(2,1)S(1)}, u32[]{:S(2)}) copy-start(bf16[128,4096]{1,0:T(8,128)(2,1)S(1)} %fusion.2.mix_ref) | copy-start | bytes 3145732
  9.8 36.0 %collective-permute-start = (bf16[128,4096]{1,0:T(8,128)(2,1)S(1)}, bf16[128,4096]{1,0:T(8,128)(2,1)}, u32[]{:S(2)}, u32[]{:S(2)}) collective-permute-start(bf16[128,4096]{1,0:T(8,128)(2,1)S(1)} %fusion.2.mix_ref), channel_id=1, source_target_pairs={{0,1},{1,2},{2,3},{4,5},{5,6},{6,7},{8,9},{9,10},{10,11},{12,13},{... | collective-permute-start | bytes 3145736 | tf_op jit(solution)/shard_map/ppermute | solution.py:316
  59.5 34.2 %copy-start.5 = (bf16[128,4096]{1,0:T(8,128)(2,1)S(1)}, bf16[128,4096]{1,0:T(8,128)(2,1)}, u32[]{:S(2)}) copy-start(bf16[128,4096]{1,0:T(8,128)(2,1)} %get-tuple-element.30) | copy-start | bytes 3145732
  59.5 28.7 %collective-permute-start.3 = (bf16[128,4096]{1,0:T(8,128)(2,1)}, bf16[128,4096]{1,0:T(8,128)(2,1)}, u32[]{:S(2)}, u32[]{:S(2)}) collective-permute-start(bf16[128,4096]{1,0:T(8,128)(2,1)} %get-tuple-element.30), channel_id=1, source_target_pairs={{1,0},{2,1},{3,2},{5,4},{6,5},{7,6},{9,8},{10,9},{11,10},{13,12},{... | collective-permute-start | bytes 3145736 | tf_op jit(solution)/shard_map/ppermute | solution.py:322
  60.9 28.6 %collective-permute-start.1 = (bf16[128,4096]{1,0:T(8,128)(2,1)}, bf16[128,4096]{1,0:T(8,128)(2,1)}, u32[]{:S(2)}, u32[]{:S(2)}) collective-permute-start(bf16[128,4096]{1,0:T(8,128)(2,1)} %get-tuple-element.30), channel_id=1, source_target_pairs={{0,1},{1,2},{2,3},{4,5},{5,6},{6,7},{8,9},{9,10},{10,11},{12,13},{... | collective-permute-start | bytes 3145736 | tf_op jit(solution)/shard_map/ppermute | solution.py:322
  88.2 27.4 %collective-permute-start.4 = (bf16[128,4096]{1,0:T(8,128)(2,1)}, bf16[128,4096]{1,0:T(8,128)(2,1)}, u32[]{:S(2)}, u32[]{:S(2)}) collective-permute-start(bf16[128,4096]{1,0:T(8,128)(2,1)} %collective-permute-done.3), channel_id=1, source_target_pairs={{1,0},{2,1},{5,4},{6,5},{9,8},{10,9},{13,12},{14,13},{17,16},{18,1... | collective-permute-start | bytes 3145736 | tf_op jit(solution)/shard_map/ppermute | solution.py:322
  89.6 26.1 %collective-permute-start.2 = (bf16[128,4096]{1,0:T(8,128)(2,1)}, bf16[128,4096]{1,0:T(8,128)(2,1)}, u32[]{:S(2)}, u32[]{:S(2)}) collective-permute-start(bf16[128,4096]{1,0:T(8,128)(2,1)} %collective-permute-done.1), channel_id=1, source_target_pairs={{1,2},{2,3},{5,6},{6,7},{9,10},{10,11},{13,14},{14,15},{17,18},{18... | collective-permute-start | bytes 3145736 | tf_op jit(solution)/shard_map/ppermute | solution.py:322
  115.7 27.2 %collective-permute-start.5 = (bf16[128,4096]{1,0:T(8,128)(2,1)}, bf16[128,4096]{1,0:T(8,128)(2,1)S(1)}, u32[]{:S(2)}, u32[]{:S(2)}) collective-permute-start(bf16[128,4096]{1,0:T(8,128)(2,1)} %collective-permute-done.4), channel_id=1, source_target_pairs={{1,0},{5,4},{9,8},{13,12},{17,16},{21,20},{25,24},{29,28}} | collective-permute-start | bytes 3145736 | tf_op jit(solution)/shard_map/ppermute | solution.py:322
  117.0 29.6 %collective-permute-start.6 = (bf16[128,4096]{1,0:T(8,128)(2,1)}, bf16[128,4096]{1,0:T(8,128)(2,1)S(1)}, u32[]{:S(2)}, u32[]{:S(2)}) collective-permute-start(bf16[128,4096]{1,0:T(8,128)(2,1)} %collective-permute-done.2), channel_id=1, source_target_pairs={{2,3},{6,7},{10,11},{14,15},{18,19},{22,23},{26,27},{30,31}} | collective-permute-start | bytes 3145736 | tf_op jit(solution)/shard_map/ppermute | solution.py:322
  130.2 16.4 %copy-start.2 = (bf16[512,4096]{1,0:T(8,128)(2,1)}, bf16[512,4096]{1,0:T(8,128)(2,1)S(1)}, u32[]{:S(2)}) copy-start(bf16[512,4096]{1,0:T(8,128)(2,1)S(1)} %fusion) | copy-start | bytes 12582916
  130.4 18.6 %collective-permute-start.8 = (bf16[128,4096]{1,0:T(8,128)(2,1)S(1)}, bf16[128,4096]{1,0:T(8,128)(2,1)S(1)}, u32[]{:S(2)}, u32[]{:S(2)}) collective-permute-start(bf16[128,4096]{1,0:T(8,128)(2,1)S(1)} %get-tuple-element.55), channel_id=1, source_target_pairs={{3,2},{7,6},{11,10},{15,14},{19,18},{23,22},{27,26},{31,30}} | collective-permute-start | bytes 3145736 | tf_op jit(solution)/shard_map/ppermute | solution.py:322
  131.2 27.0 %collective-permute-start.7 = (bf16[128,4096]{1,0:T(8,128)(2,1)S(1)}, bf16[128,4096]{1,0:T(8,128)(2,1)}, u32[]{:S(2)}, u32[]{:S(2)}) collective-permute-start(bf16[128,4096]{1,0:T(8,128)(2,1)S(1)} %get-tuple-element.56), channel_id=1, source_target_pairs={{0,1},{4,5},{8,9},{12,13},{16,17},{20,21},{24,25},{28,29}} | collective-permute-start | bytes 3145736 | tf_op jit(solution)/shard_map/ppermute | solution.py:322
  174.3 0.7 collective-permute-start.11
  178.6 50.4 %collective-permute-start.9 = (bf16[128,4096]{1,0:T(8,128)(2,1)}, bf16[128,4096]{1,0:T(8,128)(2,1)S(1)}, u32[]{:S(2)}, u32[]{:S(2)}) collective-permute-start(bf16[128,4096]{1,0:T(8,128)(2,1)} %get-tuple-element.54), channel_id=1, source_target_pairs={{0,1},{1,2},{4,5},{5,6},{8,9},{9,10},{12,13},{13,14},{16,17},{17,1... | collective-permute-start | bytes 3145736 | tf_op jit(solution)/shard_map/ppermute | solution.py:322
  209.7 42.3 %collective-permute-start.12 = (bf16[128,4096]{1,0:T(8,128)(2,1)S(1)}, bf16[128,4096]{1,0:T(8,128)(2,1)S(1)}, u32[]{:S(2)}, u32[]{:S(2)}) collective-permute-start(bf16[128,4096]{1,0:T(8,128)(2,1)S(1)} %get-tuple-element.53), channel_id=1, source_target_pairs={{1,0},{2,1},{3,2},{5,4},{6,5},{7,6},{9,8},{10,9},{11,10},{13,12},{... | collective-permute-start | bytes 3145736 | tf_op jit(solution)/shard_map/ppermute | solution.py:322
  230.5 23.4 %collective-permute-start.10 = (bf16[128,4096]{1,0:T(8,128)(2,1)S(1)}, bf16[128,4096]{1,0:T(8,128)(2,1)S(1)}, u32[]{:S(2)}, u32[]{:S(2)}) collective-permute-start(bf16[128,4096]{1,0:T(8,128)(2,1)S(1)} %add_convert_fusion.2), channel_id=1, source_target_pairs={{0,1},{1,2},{2,3},{4,5},{5,6},{6,7},{8,9},{9,10},{10,11},{12,13},{... | collective-permute-start | bytes 3145736 | tf_op jit(solution)/shard_map/ppermute | solution.py:322
  254.8 53.2 %copy-start.3 = (bf16[1,128,4096]{2,1,0:T(8,128)(2,1)S(1)}, bf16[1,128,4096]{2,1,0:T(8,128)(2,1)}, u32[]{:S(2)}) copy-start(bf16[1,128,4096]{2,1,0:T(8,128)(2,1)} %param.9) | copy-start | bytes 3145732
  274.1 33.9 %collective-permute-start.13 = (bf16[128,4096]{1,0:T(8,128)(2,1)}, bf16[128,4096]{1,0:T(8,128)(2,1)}, u32[]{:S(2)}, u32[]{:S(2)}) collective-permute-start(bf16[128,4096]{1,0:T(8,128)(2,1)} %get-tuple-element.47), channel_id=1, source_target_pairs={{1,0},{2,1},{3,2},{5,4},{6,5},{7,6},{9,8},{10,9},{11,10},{13,12},{... | collective-permute-start | bytes 3145736 | tf_op jit(solution)/shard_map/ppermute | solution.py:316
  (3 other events, 11.3 us)
Sparse Core Ops, SparseCore 0:
  9.9 93.9 all-gather.1
  172.9 118.1 reduce-scatter.1
